TPU v7x, 32 devices: a whole 2x2x4 slice. The times are simulated.
32 devices in a mesh: dp: 8 (over z, x), tensor: 4 (over y, core).
Axes of the slice: x: 2, y: 2, z: 4, core: 2. Of those that a mesh axis runs over, the one named last changes fastest.
Arguments:
- tokens: bfloat16 [9344, 768], P('dp'), may hold values from -6 to 6
- cotangent: bfloat16 [9344, 768], P('dp'), may hold values from -6 to 6
- image_group: int32 [16], replicated, may hold values from 0 to 7, as said below
- image_length: int32 [16], replicated, may hold values from 197 to 577, as said below
- first_gain: float32 [768], replicated, may hold values from 0.5 to 1.5
- first_shift: float32 [768], replicated, may hold values from -1.25 to 1.25
- qkv_weight: bfloat16 [768, 3, 768], P(None, None, 'tensor'), may hold values from -0.21875 to 0.21875
- qv_bias: float32 [2, 768], P(None, 'tensor'), may hold values from -3 to 3
- out_weight: bfloat16 [768, 768], P('tensor'), may hold values from -1.5 to 1.5
- out_bias: float32 [768], replicated, may hold values from -1.75 to 1.75
- second_gain: float32 [768], replicated, may hold values from 0.5 to 1.5
- second_shift: float32 [768], replicated, may hold values from -1.25 to 1.25
- up_weight: bfloat16 [768, 3072], P(None, 'tensor'), may hold values from -0.21875 to 0.21875
- up_bias: float32 [3072], P('tensor'), may hold values from -3 to 3
- down_weight: bfloat16 [3072, 768], P('tensor'), may hold values from -0.109375 to 0.109375
- down_bias: float32 [768], replicated, may hold values from -1.75 to 1.75
Outputs:
- block_out: bfloat16 [9344, 768], P('dp')
- input_grad: float32 [9344, 768], P('dp')
- first_gain_grad: float32 [768], replicated
- first_shift_grad: float32 [768], replicated
- qkv_weight_grad: float32 [768, 3, 768], P(None, None, 'tensor')
- qv_bias_grad: float32 [2, 768], P(None, 'tensor')
- out_weight_grad: float32 [768, 768], P('tensor')
- out_bias_grad: float32 [768], replicated
- second_gain_grad: float32 [768], replicated
- second_shift_grad: float32 [768], replicated
- up_weight_grad: float32 [768, 3072], P(None, 'tensor')
- up_bias_grad: float32 [3072], P('tensor')
- down_weight_grad: float32 [3072, 768], P('tensor')
- down_bias_grad: float32 [768], replicated
Inputs may be any that keep to these rules, and one draw needn't show every extreme that they name: `image_group`: exactly 2 images name each data group. `image_length`: every entry is 197 or 577; in every draw some data group holds 2 images of 577 tokens and another only images of 197 tokens.
All inputs are finite; a program needn't handle non-finite values.
Results may differ from a plain program's by a relative error of at most 0.018.
Values may be sent and summed in bfloat16 or wider, within the bound.
A program may use at most 128 MiB of HBM per device.

v0:
```python
import jax
import jax.numpy as jnp
from jax import lax
from jax.sharding import PartitionSpec as P

HD = 64
SLOT = 584


EPSILON = 1e-06
MASKED = -1e30


def layer_norm(token_rows, gain_row, shift_row):
    average = jnp.mean(token_rows, axis=-1, keepdims=True)
    centered = token_rows - average
    variance = jnp.mean(centered * centered, axis=-1, keepdims=True)
    return centered * lax.rsqrt(variance + EPSILON) * gain_row + shift_row


def gelu_exact(values):
    return jax.nn.gelu(values, approximate=False)


def segment_rows(image_group, image_length, group_index, row_count):
    in_group = image_group == group_index
    lengths = jnp.where(in_group, image_length, 0)
    run_ends = jnp.cumsum(lengths)
    position = jnp.arange(row_count, dtype=jnp.int32)
    finished = (position[:, None] >= run_ends[None, :]) & in_group[None, :]
    segment = jnp.sum(finished.astype(jnp.int32), axis=1)
    return (segment, position < run_ends[-1])


def image_starts(image_group, image_length, group_index, image_count):
    in_group = image_group == group_index
    lengths = jnp.where(in_group, image_length, 0)
    begins = jnp.cumsum(lengths) - lengths
    rank = jnp.cumsum(in_group.astype(jnp.int32)) - 1
    numbers = jnp.arange(image_count, dtype=jnp.int32)
    picked = in_group[None, :] & (rank[None, :] == numbers[:, None])
    return jnp.sum(jnp.where(picked, begins[None, :], 0), axis=1)


def outer_sum(left_side, right_side):
    return lax.dot_general(
        left_side, right_side, (((0,), (0,)), ((), ())), preferred_element_type=jnp.float32
    )


def times_transposed(left_side, right_side):
    return lax.dot_general(
        left_side, right_side, (((1,), (1,)), ((), ())), preferred_element_type=jnp.float32
    )


def window_scores(queries, key_heads, inside, score_scale):
    scores = (
        jnp.einsum("qhe,khe->hqk", queries, key_heads, preferred_element_type=jnp.float32)
        * score_scale
    )
    pair_mask = inside[:, None] & inside[None, :]
    return jnp.where(pair_mask[None], scores, MASKED)


def attend_window(queries, key_heads, value_heads, inside, score_scale):
    scores = window_scores(queries, key_heads, inside, score_scale)
    largest = jnp.max(scores, axis=-1, keepdims=True)
    exponent = jnp.exp(scores - largest)
    row_total = jnp.sum(exponent, axis=-1, keepdims=True)
    weights = (exponent / row_total).astype(jnp.bfloat16)
    attended = jnp.einsum("hqk,khe->qhe", weights, value_heads, preferred_element_type=jnp.float32)
    return (attended.astype(jnp.bfloat16), jnp.transpose((largest + jnp.log(row_total))[..., 0]))


def attention_forward(
    query_heads, key_heads, value_heads, segment, window_begins, slot_rows, score_scale
):
    row_count = query_heads.shape[0]
    attended_full = jnp.zeros(query_heads.shape, jnp.bfloat16)
    log_full = jnp.zeros((row_count, query_heads.shape[1]), jnp.float32)
    for image_number in range(window_begins.shape[0]):
        begin = window_begins[image_number]
        queries = lax.dynamic_slice_in_dim(query_heads, begin, slot_rows, 0)
        keys_here = lax.dynamic_slice_in_dim(key_heads, begin, slot_rows, 0)
        values_here = lax.dynamic_slice_in_dim(value_heads, begin, slot_rows, 0)
        inside = lax.dynamic_slice_in_dim(segment, begin, slot_rows, 0) == image_number
        attended, log_window = attend_window(queries, keys_here, values_here, inside, score_scale)
        previous = lax.dynamic_slice_in_dim(attended_full, begin, slot_rows, 0)
        attended_full = lax.dynamic_update_slice_in_dim(
            attended_full, jnp.where(inside[:, None, None], attended, previous), begin, 0
        )
        previous_log = lax.dynamic_slice_in_dim(log_full, begin, slot_rows, 0)
        log_full = lax.dynamic_update_slice_in_dim(
            log_full, jnp.where(inside[:, None], log_window, previous_log), begin, 0
        )
    return (attended_full, log_full)


def mlp_forward(normed_low, up_weight, up_bias, down_weight):
    pre = jnp.dot(normed_low, up_weight, preferred_element_type=jnp.float32) + up_bias
    hidden, gelu_back = jax.vjp(gelu_exact, pre)
    hidden_low = hidden.astype(jnp.bfloat16)
    return (
        jnp.dot(hidden_low, down_weight, preferred_element_type=jnp.float32),
        hidden_low,
        gelu_back,
    )


def mlp_backward(out_low, hidden_low, normed_low, gelu_back, up_weight, down_weight):
    down_grad = outer_sum(hidden_low, out_low)
    hidden_grad = times_transposed(out_low, down_weight)
    pre_low = gelu_back(hidden_grad)[0].astype(jnp.bfloat16)
    up_grad = outer_sum(normed_low, pre_low)
    up_bias_grad = jnp.sum(pre_low.astype(jnp.float32), axis=0)
    return (down_grad, up_grad, up_bias_grad, times_transposed(pre_low, up_weight))


def attn_backward(
    middle_low,
    attended,
    out_weight,
    query_heads,
    log_full,
    key_heads,
    value_heads,
    segment,
    window_begins,
    slot_rows,
    score_scale,
    normed_low,
    flat_weight,
):
    out_weight_grad = outer_sum(attended, middle_low)
    attended_grad = times_transposed(middle_low, out_weight).astype(jnp.bfloat16)
    grad_heads = attended_grad.reshape(query_heads.shape)
    query_grad = jnp.zeros(query_heads.shape, jnp.float32)
    key_grad = jnp.zeros(query_heads.shape, jnp.float32)
    value_grad = jnp.zeros(query_heads.shape, jnp.float32)
    for image_number in range(window_begins.shape[0]):
        begin = window_begins[image_number]
        queries = lax.dynamic_slice_in_dim(query_heads, begin, slot_rows, 0)
        keys_here = lax.dynamic_slice_in_dim(key_heads, begin, slot_rows, 0)
        values_here = lax.dynamic_slice_in_dim(value_heads, begin, slot_rows, 0)
        grad_block = lax.dynamic_slice_in_dim(grad_heads, begin, slot_rows, 0)
        log_block = lax.dynamic_slice_in_dim(log_full, begin, slot_rows, 0)
        inside = lax.dynamic_slice_in_dim(segment, begin, slot_rows, 0) == image_number
        scores = window_scores(queries, keys_here, inside, score_scale)
        probabilities = jnp.exp(scores - jnp.transpose(log_block)[..., None])
        value_part = jnp.einsum(
            "hqk,qhe->khe",
            probabilities.astype(jnp.bfloat16),
            grad_block,
            preferred_element_type=jnp.float32,
        )
        prob_grad = jnp.einsum(
            "qhe,khe->hqk", grad_block, values_here, preferred_element_type=jnp.float32
        )
        inner_sum = jnp.sum(probabilities * prob_grad, axis=-1, keepdims=True)
        score_grad = (probabilities * (prob_grad - inner_sum)).astype(jnp.bfloat16)
        query_part = (
            jnp.einsum("hqk,khe->qhe", score_grad, keys_here, preferred_element_type=jnp.float32)
            * score_scale
        )
        key_part = (
            jnp.einsum("hqk,qhe->khe", score_grad, queries, preferred_element_type=jnp.float32)
            * score_scale
        )
        previous = lax.dynamic_slice_in_dim(query_grad, begin, slot_rows, 0)
        query_grad = lax.dynamic_update_slice_in_dim(
            query_grad, jnp.where(inside[:, None, None], query_part, previous), begin, 0
        )
        key_grad = lax.dynamic_update_slice_in_dim(
            key_grad, lax.dynamic_slice_in_dim(key_grad, begin, slot_rows, 0) + key_part, begin, 0
        )
        value_grad = lax.dynamic_update_slice_in_dim(
            value_grad,
            lax.dynamic_slice_in_dim(value_grad, begin, slot_rows, 0) + value_part,
            begin,
            0,
        )
    row_count = key_heads.shape[0]
    shard_width = key_heads.shape[1] * key_heads.shape[2]
    query_low = query_grad.reshape(row_count, shard_width).astype(jnp.bfloat16)
    key_low = key_grad.reshape(row_count, shard_width).astype(jnp.bfloat16)
    value_low = value_grad.reshape(row_count, shard_width).astype(jnp.bfloat16)
    joined_grad = jnp.concatenate([query_low, key_low, value_low], axis=1)
    qkv_grad = outer_sum(normed_low, joined_grad).reshape(flat_weight.shape[0], 3, shard_width)
    qv_bias_grad = jnp.stack(
        [
            jnp.sum(query_low.astype(jnp.float32), axis=0),
            jnp.sum(value_low.astype(jnp.float32), axis=0),
        ]
    )
    return (out_weight_grad, qkv_grad, qv_bias_grad, times_transposed(joined_grad, flat_weight))


def body(
    tokens,
    cotangent,
    image_group,
    image_length,
    first_gain,
    first_shift,
    qkv_weight,
    qv_bias,
    out_weight,
    out_bias,
    second_gain,
    second_shift,
    up_weight,
    up_bias,
    down_weight,
    down_bias,
):
    row_count, model_width = tokens.shape
    shard_width = qkv_weight.shape[2]
    heads_local = shard_width // HD
    image_count = row_count // SLOT
    score_scale = HD ** (-0.5)
    group_index = lax.axis_index("dp")
    segment, is_valid = segment_rows(image_group, image_length, group_index, row_count)
    window_begins = jnp.minimum(
        image_starts(image_group, image_length, group_index, image_count), row_count - SLOT
    )
    valid_rows = is_valid.astype(jnp.float32)[:, None]
    token_rows = tokens.astype(jnp.float32)
    normed, first_back = jax.vjp(layer_norm, token_rows, first_gain, first_shift)
    normed_low = normed.astype(jnp.bfloat16)
    flat_weight = qkv_weight.reshape(model_width, 3 * shard_width)
    projected = jnp.dot(normed_low, flat_weight, preferred_element_type=jnp.float32)
    head_shape = (row_count, heads_local, HD)
    query_heads = (projected[:, :shard_width] + qv_bias[0]).astype(jnp.bfloat16).reshape(head_shape)
    key_heads = projected[:, shard_width : 2 * shard_width].astype(jnp.bfloat16).reshape(head_shape)
    value_heads = (
        (projected[:, 2 * shard_width :] + qv_bias[1]).astype(jnp.bfloat16).reshape(head_shape)
    )
    attended_heads, log_full = attention_forward(
        query_heads, key_heads, value_heads, segment, window_begins, SLOT, score_scale
    )
    attended = attended_heads.reshape(row_count, shard_width)
    attn_partial = jnp.dot(attended, out_weight, preferred_element_type=jnp.float32)
    out_grad = cotangent.astype(jnp.float32) * valid_rows
    out_low = out_grad.astype(jnp.bfloat16)
    down_bias_grad = jnp.sum(out_grad, axis=0)
    middle = (
        token_rows
        + lax.psum(attn_partial.astype(jnp.bfloat16), "tensor").astype(jnp.float32)
        + out_bias
    )
    normed_two, second_back = jax.vjp(layer_norm, middle, second_gain, second_shift)
    normed_two_low = normed_two.astype(jnp.bfloat16)
    mlp_partial, hidden_low, gelu_back = mlp_forward(
        normed_two_low, up_weight, up_bias, down_weight
    )
    mlp_total = lax.psum(mlp_partial.astype(jnp.bfloat16), "tensor").astype(jnp.float32)
    block_out = ((middle + mlp_total + down_bias) * valid_rows).astype(jnp.bfloat16)
    down_grad, up_grad, up_bias_grad, normed_two_part = mlp_backward(
        out_low, hidden_low, normed_two_low, gelu_back, up_weight, down_weight
    )
    normed_two_grad = lax.psum(normed_two_part.astype(jnp.bfloat16), "tensor").astype(jnp.float32)
    middle_norm_grad, second_gain_grad, second_shift_grad = second_back(normed_two_grad)
    middle_grad = out_grad + middle_norm_grad
    out_bias_grad = jnp.sum(middle_grad, axis=0)
    out_weight_grad, qkv_grad, qv_bias_grad, normed_part = attn_backward(
        middle_grad.astype(jnp.bfloat16),
        attended,
        out_weight,
        query_heads,
        log_full,
        key_heads,
        value_heads,
        segment,
        window_begins,
        SLOT,
        score_scale,
        normed_low,
        flat_weight,
    )
    normed_grad = lax.psum(normed_part.astype(jnp.bfloat16), "tensor").astype(jnp.float32)
    input_norm_grad, first_gain_grad, first_shift_grad = first_back(normed_grad)
    input_grad = input_norm_grad + middle_grad
    summed = lax.psum(
        (
            first_gain_grad,
            first_shift_grad,
            qkv_grad,
            qv_bias_grad,
            out_weight_grad,
            out_bias_grad,
            second_gain_grad,
            second_shift_grad,
            up_grad,
            up_bias_grad,
            down_grad,
            down_bias_grad,
        ),
        "dp",
    )
    return (block_out, input_grad) + tuple(summed)


def solution(mesh):
    in_specs = (
        P("dp", None),
        P("dp", None),
        P(),
        P(),
        P(),
        P(),
        P(None, None, "tensor"),
        P(None, "tensor"),
        P("tensor", None),
        P(),
        P(),
        P(),
        P(None, "tensor"),
        P("tensor"),
        P("tensor", None),
        P(),
    )
    out_specs = (
        P("dp", None),
        P("dp", None),
        P(),
        P(),
        P(None, None, "tensor"),
        P(None, "tensor"),
        P("tensor", None),
        P(),
        P(),
        P(),
        P(None, "tensor"),
        P("tensor"),
        P("tensor", None),
        P(),
    )
    return jax.shard_map(body, mesh=mesh, in_specs=in_specs, out_specs=out_specs, check_vma=False)
```

profile of v0, /device:TPU:0, one launch (start us, length us, event | category | flops | bytes accessed | tf_op | source)
XLA Modules:
  0.0 553.0 jit_solution(11607171620120785651)
XLA Ops:
  13.4 1.9 convert_reduce_fusion.2
  15.2 2.2 fusion.13
  17.5 1.5 fusion.115
  19.0 1.6 copy-done.19
  22.4 1.7 fusion.62
  28.9 1.7 fusion.60
  30.7 3.8 dynamic_update_slice.30
  34.5 4.2 fusion.58
  38.7 4.2 dynamic_update_slice.31
  42.9 2.9 convolution_convert_fusion.1
  45.8 10.9 %all-reduce.10.cloned.1.call-start = ((), (), s32[]{:S(2)}) async-start(), calls=%async_computation.1 | async-start | bytes 3588096 | tf_op jit(solution)/shard_map/psum | solution.py:262
  57.9 36.9 %all-reduce.8.cloned.1.call-done = bf16[1168,768]{1,0:T(8,128)(2,1)} async-done(((bf16[1168,768]{1,0:T(8,128)(2,1)}), bf16[1168,768]{1,0:T(8,128)(2,1)}) %all-reduce.8.cloned.1.call-update) | async-done | bytes 1794064 | tf_op jit(solution)/shard_map/psum | solution.py:249
  94.8 2.3 fusion.29
  98.1 10.5 %multiply_convert_fusion.3 = (bf16[1168,768]{1,0:T(8,128)(2,1)}, f32[1168,768]{1,0:T(8,128)S(1)}, f32[1168,768]{1,0:T(8,128)S(1)}) fusion(f32[768]{0:T(1024)S(1)} %copy-done.45, bf16[768,768]{1,0:T(8,128)(2,1)S(1)} %copy-done, f32[768]{0:T(1024)S(1)} %copy-done.46, f32[768]{0:T(1024)S(1)} %copy-done.33, f32[1168]{0:T(1024)S(1)} %fusion.94, ...), kind=kOutput, calls=%fused_computation.52 | convolution fusion | flops 1445105664 | bytes 13759616 | tf_op jit(solution)/shard_map/dot_general | solution.py:101
  108.6 3.4 convert_reduce_fusion.3
  113.4 2.8 convolution_convert_fusion.2
  118.6 4.6 convolution_convert_fusion.3
  123.2 39.8 %all-reduce.10.cloned.1.call-done = bf16[1168,768]{1,0:T(8,128)(2,1)} async-done(((bf16[1168,768]{1,0:T(8,128)(2,1)}), bf16[1168,768]{1,0:T(8,128)(2,1)}) %all-reduce.10.cloned.1.call-update) | async-done | bytes 1794064 | tf_op jit(solution)/shard_map/psum | solution.py:262
  162.9 3.7 convert_reduce_fusion.1
  166.6 2.9 fusion.17
  169.6 2.7 fusion.119
  176.0 1.4 fusion.52
  177.5 1.6 fusion.49
  179.1 1.6 fusion.39
  181.9 2.4 multiply_convert_fusion
  184.4 2.9 dynamic_update_slice.34
  187.4 3.1 fusion.53
  190.5 3.2 dynamic_update_slice.35
  194.6 2.9 dynamic_update_slice.36
  197.6 3.3 fusion.54
  200.9 3.2 dynamic_update_slice.37
  205.0 2.9 dynamic_update_slice.38
  208.0 4.0 fusion.45
  211.9 3.4 dynamic_update_slice.39
  216.3 4.3 convolution_convert_fusion
  220.7 5.4 fusion.66
  226.1 3.7 fusion.113
  229.8 1.4 fusion.63
  231.3 2.7 fusion.72
  234.2 63.1 %all-reduce.14.cloned.1.call-done = (bf16[1168,768]{1,0:T(8,128)(2,1)}, bf16[1168,768]{1,0:T(8,128)(2,1)}) async-done(((bf16[1168,768]{1,0:T(8,128)(2,1)}, bf16[1168,768]{1,0:T(8,128)(2,1)}), (bf16[1168,768]{1,0:T(8,128)(2,1)}, bf16[1168,768]{1,0:T(8,128)(2,1)})) %all-reduce.14.cloned.1.call-update) | async-done | bytes 3588112 | tf_op jit(solution)/shard_map/psum | solution.py:257
  297.4 2.9 convert_reduce_fusion
  300.3 2.4 fusion.18
  302.7 39.7 %all-reduce = (f32[768]{0:T(1024)}, f32[768]{0:T(1024)}, f32[2,192]{1,0:T(2,128)}, f32[768]{0:T(1024)}, f32[768]{0:T(1024)}, /*index=5*/f32[768]{0:T(1024)}, f32[768]{0:T(1024)}, f32[768]{0:T(1024)}) all-reduce(f32[768]{0:T(1024)S(1)} %get-tuple-element.16, ...), channel_id=1, replica_groups=mesh['dp'=8,'tensor'=4] {'dp'}, use_global_device_ids=true, to_apply=%region_23.24 | all-reduce | flops 5760 | bytes 46080 | tf_op jit(solution)/shard_map/psum | solution.py:284
  342.4 6.3 %add_add_fusion.2 = (f32[1168,768]{1,0:T(8,128)}, bf16[1168,768]{1,0:T(8,128)(2,1)}) fusion(f32[1168,768]{1,0:T(8,128)} %copy-done.8, bf16[1168,768]{1,0:T(8,128)(2,1)S(1)} %copy-done.2, bf16[1168,768]{1,0:T(8,128)(2,1)} %get-tuple-element.35, f32[1168]{0:T(1024)S(1)} %negate_multiply_fusion.1, f32[1168]{0:T(1024)S(1)} %multiply_multiply_fusion.5, ...), kind=kLoop, calls=%fused_computation.45 | loop fusion | flops 16146432 | bytes 16179008 | tf_op jit(solution)/shard_map/add | solution.py:283
  348.8 190.9 %all-reduce.12.cloned.1.call-done = (f32[768,3,192]{0,2,1:T(8,128)}, f32[192,768]{1,0:T(8,128)}, f32[768,768]{1,0:T(8,128)}, f32[768,768]{1,0:T(8,128)}) async-done(((f32[768,3,192]{0,2,1:T(8,128)}, f32[192,768]{1,0:T(8,128)}, f32[768,768]{1,0:T(8,128)}, f32[768,768]{1,0:T(8,128)}), (f32[768,3,192]{0,2,1:T(8,128)}, f32[192,768]{1,0:T(8,128)}, f32[768,768]{1,0:T(8,128)}, ...) | async-done | bytes 7077904 | tf_op jit(solution)/shard_map/psum | solution.py:284
  539.7 2.9 copy.86
  543.5 1.4 copy.88
  544.9 1.4 copy.89
  (173 shorter events, 23.6 us)
Async XLA Ops:
  7.2 90.9 %copy-start = (bf16[768,768]{1,0:T(8,128)(2,1)S(1)}, bf16[768,768]{1,0:T(8,128)(2,1)}, u32[]{:S(2)}) copy-start(bf16[768,768]{1,0:T(8,128)(2,1)} %param.28) | copy-start | bytes 3538948
  7.2 10.2 %copy-start.2 = (bf16[1168,768]{1,0:T(8,128)(2,1)S(1)}, bf16[1168,768]{1,0:T(8,128)(2,1)}, u32[]{:S(2)}) copy-start(bf16[1168,768]{1,0:T(8,128)(2,1)} %param.16) | copy-start | bytes 5382148
  7.2 10.2 %copy-start.42 = (f32[2,192]{1,0:T(2,128)S(1)}, f32[2,192]{1,0:T(2,128)}, u32[]{:S(2)}) copy-start(f32[2,192]{1,0:T(2,128)} %param.23) | copy-start | bytes 4612
  7.2 10.2 %copy-start.34 = (f32[768]{0:T(1024)S(1)}, f32[768]{0:T(1024)}, u32[]{:S(2)}) copy-start(f32[768]{0:T(1024)} %param.20) | copy-start | bytes 9220
  7.2 10.2 %copy-start.48 = (f32[768]{0:T(1024)S(1)}, f32[768]{0:T(1024)}, u32[]{:S(2)}) copy-start(f32[768]{0:T(1024)} %param.21) | copy-start | bytes 9220
  7.2 87.5 %all-reduce.8.cloned.1.call-start = ((), (), s32[]{:S(2)}) async-start(), calls=%async_computation | async-start | bytes 3588096 | tf_op jit(solution)/shard_map/psum | solution.py:249
  13.3 4.2 copy-start.44
  20.6 4.8 copy-start.14
  22.0 6.1 %copy-start.38 = (pred[584]{0:T(1024)(128)(4,1)}, pred[584]{0:T(1024)(128)(4,1)S(1)}, u32[]{:S(2)}) copy-start(pred[584]{0:T(1024)(128)(4,1)S(1)} %get-tuple-element.54) | copy-start | bytes 1756
  22.0 12.5 %copy-start.36 = (pred[584]{0:T(1024)(128)(4,1)}, pred[584]{0:T(1024)(128)(4,1)S(1)}, u32[]{:S(2)}) copy-start(pred[584]{0:T(1024)(128)(4,1)S(1)} %get-tuple-element.53) | copy-start | bytes 1756
  24.1 2.6 copy-start.12
  24.1 4.0 copy-start.20
  26.7 2.2 copy-start.4
  27.4 7.0 %copy-start.32 = (f32[3,584]{1,0:T(4,128)}, f32[3,584]{1,0:T(4,128)S(1)}, u32[]{:S(2)}) copy-start(f32[3,584]{1,0:T(4,128)S(1)} %fusion.9) | copy-start | bytes 21028
  28.1 2.5 copy-start.31
  38.7 56.1 %copy-start.30 = (f32[768]{0:T(1024)S(1)}, f32[768]{0:T(1024)}, u32[]{:S(2)}) copy-start(f32[768]{0:T(1024)} %param.25) | copy-start | bytes 9220
  45.8 117.2 %all-reduce.10.cloned.1.call-start = ((), (), s32[]{:S(2)}) async-start(), calls=%async_computation.1 | async-start | bytes 3588096 | tf_op jit(solution)/shard_map/psum | solution.py:262
  57.9 40.2 %copy-start.33 = (f32[768]{0:T(1024)S(1)}, f32[768]{0:T(1024)}, u32[]{:S(2)}) copy-start(f32[768]{0:T(1024)} %param.26) | copy-start | bytes 9220
  94.8 2.3 copy-start.5
  94.8 3.3 copy-start.45
  94.8 3.3 copy-start.46
  98.1 10.5 %copy-start.22 = (bf16[1168,768]{1,0:T(8,128)(2,1)S(1)}, bf16[1168,768]{1,0:T(8,128)(2,1)}, u32[]{:S(2)}) copy-start(bf16[1168,768]{1,0:T(8,128)(2,1)} %param.17) | copy-start | bytes 5382148
  98.1 10.5 %copy-start.43 = (bf16[768,768]{1,0:T(8,128)(2,1)S(1)}, bf16[768,768]{1,0:T(8,128)(2,1)}, u32[]{:S(2)}) copy-start(bf16[768,768]{1,0:T(8,128)(2,1)} %param.30) | copy-start | bytes 3538948
  116.2 181.2 %all-reduce.14.cloned.1.call-start = ((), (), s32[]{:S(2)}) async-start(), calls=%async_computation.3 | async-start | bytes 7176192 | tf_op jit(solution)/shard_map/psum | solution.py:257
  162.9 3.7 copy-start.6
  162.9 3.7 copy-start.10
  166.6 3.0 copy-start.23
  166.6 6.5 %slice-start.2 = ((s8[4485120]{0:T(1024)(128)(4,1)}), s8[4194304]{0:T(1024)(128)(4,1)S(1)}, s32[]{:S(2)}) async-start(s8[4485120]{0:T(1024)(128)(4,1)} %bitcast.71), calls=%async_computation.6 | async-start | bytes 8388608
  169.6 2.7 copy-start.24
  169.6 3.5 slice-start.3
  172.3 2.6 copy-start.8
  173.1 7.6 %copy-start.16 = (bf16[1168,192]{0,1:T(8,128)(2,1)}, bf16[1168,192]{0,1:T(8,128)(2,1)S(1)}, u32[]{:S(2)}) copy-start(bf16[1168,192]{0,1:T(8,128)(2,1)S(1)} %convolution_convert_fusion.4) | copy-start | bytes 1345540
  175.0 2.5 copy-start.13
  176.0 4.6 slice-start
  177.5 3.2 slice-start.1
  181.9 5.4 copy-start.37
  220.6 5.5 copy-start.47
  220.6 319.1 %all-reduce.12.cloned.1.call-start = ((), (), s32[]{:S(2)}) async-start(), calls=%async_computation.2 | async-start | bytes 14155776 | tf_op jit(solution)/shard_map/psum | solution.py:284
  220.6 5.5 copy-start.7
  220.6 5.4 copy-start.51
  226.1 3.7 copy-start.9
  297.4 2.9 copy-start.11
  297.4 5.3 copy-start.40
  297.4 45.1 %copy-start.41 = (f32[768]{0:T(1024)S(1)}, f32[768]{0:T(1024)}, u32[]{:S(2)}) copy-start(f32[768]{0:T(1024)} %param.31) | copy-start | bytes 9220
  539.7 3.0 copy-start.25
  539.7 3.8 copy-start.18
  542.7 2.2 copy-start.17
  542.7 3.6 copy-start.1
  (12 other events, 16.6 us)
Sparse Core Ops, SparseCore 0:
  45.9 48.8 all-reduce.7
  116.3 46.5 all-reduce.9
  220.7 76.6 all-reduce.13
  303.4 236.2 all-reduce.11
where the time goes:
time: 562 us; the launch traced here: 553 us
  waiting for transfers between devices  331 us (59%)
  matrix products  69.9 us (12%)
  other arithmetic  41.8 us (7%)
  local copies, waits for them, and re-layouts  41.1 us (7%)
  blocking collectives  39.7 us (7%)
  between operations  18.7 us (3%)
  starting transfers between devices  11.1 us (2%)
    psum x1, waiting for transfers between devices, body(): lax.psum((first_gain_grad, first_shift_grad, qkv_grad, qv_bias_grad, out_...  191 us
    psum x1, waiting for transfers between devices, body(): lax.psum(mlp_partial.astype(jnp.bfloat16), 'tensor').astype(jnp.float32)  63.1 us
    psum x1, waiting for transfers between devices, body(): lax.psum(normed_two_part.astype(jnp.bfloat16), 'tensor').astype(jnp.float32)  39.8 us
    psum x1, blocking collectives, body(): lax.psum((first_gain_grad, first_shift_grad, qkv_grad, qv_bias_grad, out_...  39.7 us
    psum x1, waiting for transfers between devices, body(): lax.psum(attn_partial.astype(jnp.bfloat16), 'tensor').astype(jnp.float32)  36.9 us
    dot_general x4, matrix products, outer_sum(): lax.dot_general(left_side, right_side, (((0,), (0,)), ((), ())), preferre...  13.3 us
    unnamed x116, local copies, waits for them, and re-layouts  12 us
    reduce_sum x4, other arithmetic, layer_norm(): return centered * lax.rsqrt(variance + EPSILON) * gain_row + shift_row  11.9 us
  transfers between devices with their start and end apart: 4, of which 4 were waited for; matrix products, arithmetic and copies ran while one was open for 6% of the time, Pallas kernels for 0%

commit v1 on v0

v1 whole, which is shorter than its diff:
```python
import functools

import jax
import jax.numpy as jnp
from jax import lax
from jax.experimental import pallas as pl
from jax.experimental.pallas import tpu as pltpu
from jax.sharding import PartitionSpec as P

HD = 64
RES_SMALL = 197
RES_LARGE = 577
SLOT = 608
HALF = 304
EPS = 1e-06
MASKED = -1e30
BF = jnp.bfloat16
F32 = jnp.float32
MESH = pl.DeviceIdType.MESH


def dot_nn(a, b):
    return lax.dot_general(a, b, (((1,), (0,)), ((), ())), preferred_element_type=F32)


def dot_nt(a, b):
    return lax.dot_general(a, b, (((1,), (1,)), ((), ())), preferred_element_type=F32)


def dot_tn(a, b):
    return lax.dot_general(a, b, (((0,), (0,)), ((), ())), preferred_element_type=F32)


def normalize(x):
    mean = jnp.mean(x, axis=-1, keepdims=True)
    centered = x - mean
    var = jnp.mean(centered * centered, axis=-1, keepdims=True)
    scale = lax.rsqrt(var + EPS)
    return centered * scale, scale


def norm_back(u, xn, scale):
    return scale * (
        u
        - jnp.mean(u, axis=-1, keepdims=True)
        - xn * jnp.mean(u * xn, axis=-1, keepdims=True)
    )


def fold8(x):
    return jnp.sum(x.reshape(x.shape[0] // 8, 8, x.shape[1]), axis=0)


def flip(index, stride):
    return index + stride - 2 * stride * ((index // stride) % 2)


def layer_kernel(
    n_dp,
    lens,
    tok,
    cot,
    wqkv,
    wout,
    wup,
    wdown,
    g1,
    b1,
    ob,
    g2,
    b2,
    db,
    ub,
    qvb,
    block_o,
    ingrad_o,
    grads_o,
    small_o,
    normed,
    qkv,
    att,
    probs,
    normed2,
    hidden,
    pregrad,
    middle,
    midgrad,
    mg,
    agrad,
    dqkv,
    dacc,
    tmp_a,
    tmp_b,
    acc,
    accv,
    csend,
    crecv,
    ysend,
    yrecv,
    gbuf,
    rs0,
    rs1,
    rs2,
    rx,
    smc,
    smr,
    c_send,
    c_recv,
    y_send,
    y_recv,
    g_send,
    g_recv,
    d_send,
    d_recv,
    s_send,
    s_recv,
):
    levels = n_dp.bit_length() - 1
    scat = min(3, levels)
    d = lax.axis_index("dp")
    t = lax.axis_index("tensor")
    core = t % 2
    core_peer = (d, flip(t, 1))
    y_peer = (d, flip(t, 2))

    def dp_peer(level):
        return (flip(d, 2**level), t)

    bar = pltpu.get_barrier_semaphore()
    peers = [core_peer, y_peer] + [dp_peer(i) for i in range(levels)]
    for peer in peers:
        pl.semaphore_signal(bar, inc=1, device_id=peer, device_id_type=MESH)
    pl.semaphore_wait(bar, len(peers))

    own = pl.multiple_of(core * HALF, 16)
    other = pl.multiple_of((1 - core) * HALF, 16)
    width = tok.shape[1]
    heads = wout.shape[0] // HD
    rows16 = HALF // 16
    lane_head = lax.broadcasted_iota(jnp.int32, (1, wout.shape[0]), 1) // HD

    def slot_rows(s, off, size):
        return pl.ds(pl.multiple_of(s * SLOT + off, 16), size)

    def remote(src, dst, send, recv, peer):
        return pltpu.make_async_remote_copy(
            src_ref=src, dst_ref=dst, send_sem=send, recv_sem=recv, device_id=peer, device_id_type=MESH
        )

    def c_copy(s, k):
        return remote(csend, crecv.at[s, k], c_send.at[s, k], c_recv.at[s, k], core_peer)

    def y_copy(s, k):
        return remote(ysend.at[s, k], yrecv.at[s, k], y_send.at[s, k], y_recv.at[s, k], y_peer)

    def gather_copy(ref, s, k):
        region = slot_rows(s, own, HALF)
        return remote(ref.at[region], ref.at[region], g_send.at[s, k], g_recv.at[s, k], core_peer)

    def stage(s, k, part):
        csend[...] = part(other).astype(BF)
        copy = c_copy(s, k)
        copy.start()
        tmp_a[...] = part(own)
        copy.wait()

        def add(i, carry):
            r = pl.ds(pl.multiple_of(i * 16, 16), 16)
            ysend[s, k, r, :] = (tmp_a[r, :] + crecv[s, k, r, :].astype(F32)).astype(BF)
            return carry

        lax.fori_loop(0, rows16, add, 0)
        y_copy(s, k).start()

    def total(s, k, r):
        return ysend[s, k, r, :].astype(F32) + yrecv[s, k, r, :].astype(F32)

    step = [768 >> (i + 1) for i in range(scat)]

    def bit(level):
        return (d // 2**level) % 2

    def base(level):
        off = 0
        for i in range(level):
            off = off + bit(i) * step[i]
        return off

    rs = [rs0, rs1, rs2]

    def dp_rs(p, i):
        src = pl.ds(pl.multiple_of(base(i) + (1 - bit(i)) * step[i], 16), step[i])
        return remote(gbuf.at[p, src], rs[i].at[p], d_send.at[p, i], d_recv.at[p, i], dp_peer(i))

    def dp_add(p, i):
        dp_rs(p, i).wait()
        off = base(i) + bit(i) * step[i]
        out = grads_o if i == scat - 1 else gbuf

        def add(j, carry):
            r = pl.ds(pl.multiple_of(off + j * 32, 16), 32)
            rr = pl.ds(pl.multiple_of(j * 32, 16), 32)
            out[p, r, :] = (gbuf[p, r, :].astype(F32) + rs[i][p, rr, :].astype(F32)).astype(BF)
            return carry

        lax.fori_loop(0, step[i] // 32, add, 0)
        if i + 1 < scat:
            dp_rs(p, i + 1).start()

    def dp_extra(p):
        size = step[scat - 1]
        mine = pl.ds(pl.multiple_of(base(scat), 16), size)
        for e in range(levels - scat):
            copy = remote(
                grads_o.at[p, mine], rx.at[e, p], d_send.at[p, 6 + e], d_recv.at[p, 6 + e], dp_peer(scat + e)
            )
            copy.start()
            copy.wait()
            grads_o[p, mine, :] = (grads_o[p, mine, :].astype(F32) + rx[e, p].astype(F32)).astype(BF)

    def dp_ag(p, i):
        region = pl.ds(pl.multiple_of(base(i + 1), 16), step[i])
        return remote(
            grads_o.at[p, region], grads_o.at[p, region], d_send.at[p, 3 + i], d_recv.at[p, 3 + i], dp_peer(i)
        )

    def dp_last(p):
        dp_add(p, scat - 1)
        dp_extra(p)
        dp_ag(p, scat - 1).start()

    def dp_gather(p, i):
        dp_ag(p, i).wait()
        if i > 0:
            dp_ag(p, i - 1).start()

    acc[...] = jnp.zeros_like(acc)
    accv[...] = jnp.zeros_like(accv)

    def forward_attention(s, carry):
        def norm_rows(i, carry):
            r = slot_rows(s, i * 32, 32)
            xn, _ = normalize(tok[r, :].astype(F32))
            normed[r, :] = (xn * g1[...] + b1[...]).astype(BF)
            return carry

        lax.fori_loop(0, SLOT // 32, norm_rows, 0)

        def project(i, carry):
            r = slot_rows(s, i * HALF, HALF)
            x = normed[r, :]
            qkv[0, r, :] = (dot_nn(x, wqkv[0]) + qvb[0:1, :]).astype(BF)
            qkv[1, r, :] = dot_nn(x, wqkv[1]).astype(BF)
            qkv[2, r, :] = (dot_nn(x, wqkv[2]) + qvb[1:2, :]).astype(BF)
            return carry

        lax.fori_loop(0, 2, project, 0)
        whole = slot_rows(s, 0, SLOT)
        length = jnp.where(s == 0, lens[0], lens[1])
        key_bias = jnp.where(lax.broadcasted_iota(jnp.int32, (1, SLOT), 1) < length, 0.0, MASKED)

        def attend(i, carry):
            r = slot_rows(s, i * HALF, HALF)
            for h in range(heads):
                q = jnp.where(lane_head == h, qkv[0, r, :] * HD**-0.5, 0.0).astype(BF)
                scores = dot_nt(q, qkv[1, whole, :]) + key_bias
                exps = jnp.exp(scores - jnp.max(scores, axis=-1, keepdims=True))
                weights = (exps * (1.0 / jnp.sum(exps, axis=-1, keepdims=True))).astype(BF)
                probs[s * heads + h, pl.ds(pl.multiple_of(i * HALF, 16), HALF), :] = weights
                part = dot_nn(weights, qkv[2, whole, :])
                result = part if h == 0 else jnp.where(lane_head == h, part, result)
            att[r, :] = result.astype(BF)
            return carry

        lax.fori_loop(0, 2, attend, 0)
        stage(s, 0, lambda off: dot_nn(att[slot_rows(s, off, HALF), :], wout[...]))
        return carry

    lax.fori_loop(0, 2, forward_attention, 0)

    def second_norm(s):
        y_copy(s, 0).wait()

        def rows(i, carry):
            r = pl.ds(pl.multiple_of(i * 16, 16), 16)
            g = slot_rows(s, own + i * 16, 16)
            m = total(s, 0, r) + tok[g, :].astype(F32) + ob[...]
            middle[s, r, :] = m
            xn, _ = normalize(m)
            normed2[g, :] = (xn * g2[...] + b2[...]).astype(BF)
            return carry

        lax.fori_loop(0, rows16, rows, 0)
        gather_copy(normed2, s, 0).start()

    def feed_forward(s, carry):
        second_norm(s)
        gather_copy(normed2, s, 0).wait()

        def half(i, carry):
            r = slot_rows(s, i * HALF, HALF)
            tmp_a[...] = dot_nn(normed2[r, :], wup[...])
            tmp_b[...] = dot_nt(cot[r, :], wdown[...])

            def rows(j, sums):
                rr = pl.ds(pl.multiple_of(j * 16, 16), 16)
                g = slot_rows(s, i * HALF + j * 16, 16)
                x = tmp_a[rr, :] + ub[...]
                phi = 0.5 + 0.5 * lax.erf(x * 0.7071067811865476)
                hidden[g, :] = (x * phi).astype(BF)
                slope = phi + x * (jnp.exp(x * x * -0.5) * 0.3989422804014327)
                low = (tmp_b[rr, :] * slope).astype(BF)
                pregrad[g, :] = low
                return sums + fold8(low.astype(F32))

            acc[6] += lax.fori_loop(0, rows16, rows, jnp.zeros((8, width), F32))
            return carry

        lax.fori_loop(0, 2, half, 0)
        stage(s, 1, lambda off: dot_nt(pregrad[slot_rows(s, off, HALF), :], wup[...]))
        return carry

    lax.fori_loop(0, 2, feed_forward, 0)

    def weight_grad(p, left, right):
        size = step[0] if scat else 768
        for mine in (0, 1):
            off = pl.multiple_of((bit(0) if mine else 1 - bit(0)) * size, 128)
            for part in range(2):
                o = pl.multiple_of(off + part * (size // 2), 64)
                gbuf[p, pl.ds(o, size // 2), :] = dot_tn(
                    left[:, pl.ds(pl.multiple_of(off, 128), size)][:, part * (size // 2) : (part + 1) * (size // 2)],
                    right[...],
                ).astype(BF)
            if not mine:
                dp_rs(p, 0).start()

    weight_grad(0, hidden, cot)
    weight_grad(1, normed2, pregrad)

    def feed_forward_out(s, carry):
        stage(s, 2, lambda off: dot_nn(hidden[slot_rows(s, off, HALF), :], wdown[...]))
        return carry

    lax.fori_loop(0, 2, feed_forward_out, 0)

    def second_back(s):
        y_copy(s, 1).wait()

        def rows(i, sums):
            r = pl.ds(pl.multiple_of(i * 16, 16), 16)
            g = slot_rows(s, own + i * 16, 16)
            n = total(s, 1, r)
            xn, scale = normalize(middle[s, r, :])
            og = cot[g, :].astype(F32)
            m = og + norm_back(n * g2[...], xn, scale)
            midgrad[s, r, :] = m
            mg[g, :] = m.astype(BF)
            return tuple(a + fold8(b) for a, b in zip(sums, (n * xn, n, m, og), strict=True))

        zero = jnp.zeros((8, width), F32)
        sums = lax.fori_loop(0, rows16, rows, (zero,) * 4)
        for i in range(4):
            acc[2 + i] += sums[i]
        gather_copy(mg, s, 1).start()

    def attention_back(s, services):
        second_back(s)
        services[0]()
        gather_copy(mg, s, 1).wait()
        whole = slot_rows(s, 0, SLOT)
        agrad[whole, :] = dot_nt(mg[whole, :], wout[...]).astype(BF)
        dacc[...] = jnp.zeros_like(dacc)

        def chunk(i, carry):
            r = slot_rows(s, i * HALF, HALF)
            for h in range(heads):
                mask = lane_head == h
                do = agrad[r, :]
                w = probs[s * heads + h, pl.ds(pl.multiple_of(i * HALF, 16), HALF), :]
                prob_grad = dot_nt(jnp.where(mask, do, 0.0).astype(BF), qkv[2, whole, :])
                p = w.astype(F32)
                inner = jnp.sum(p * prob_grad, axis=-1, keepdims=True)
                score_grad = (p * (prob_grad - inner)).astype(BF)
                part = dot_nn(score_grad, qkv[1, whole, :])
                dq = part if h == 0 else jnp.where(mask, part, dq)
                dacc[0] += jnp.where(mask, dot_tn(score_grad, qkv[0, r, :]), 0.0)
                dacc[1] += jnp.where(mask, dot_tn(w, do), 0.0)
            low = (dq * HD**-0.5).astype(BF)
            dqkv[0, r, :] = low
            accv[0] += fold8(low.astype(F32))
            return carry

        lax.fori_loop(0, 2, chunk, 0)
        services[1]()
        dqkv[1, whole, :] = (dacc[0] * HD**-0.5).astype(BF)
        low = dacc[1].astype(BF)
        dqkv[2, whole, :] = low
        accv[1] += fold8(low.astype(F32))

        def part(off):
            r = slot_rows(s, off, HALF)
            return (
                dot_nt(dqkv[0, r, :], wqkv[0]) + dot_nt(dqkv[1, r, :], wqkv[1]) + dot_nt(dqkv[2, r, :], wqkv[2])
            )

        stage(s, 3, part)
        services[2]()

    def serve(*calls):
        def run():
            for f, p, i in calls:
                f(p, i)

        return run

    nothing = serve()
    full = scat == 3
    attention_back(0, (nothing, serve((dp_add, 0, 0)) if full else nothing, nothing))
    attention_back(
        1,
        (
            serve((dp_add, 1, 0)) if full else nothing,
            serve((dp_add, 0, 1)) if full else nothing,
            nothing,
        ),
    )

    third = wout.shape[0]
    gbuf[2, 0:third, :] = dot_tn(att[...], mg[...]).astype(BF)
    for j in range(3):
        gbuf[2, (j + 1) * third : (j + 2) * third, :] = dot_tn(dqkv[j], normed[...]).astype(BF)
    if scat:
        dp_rs(2, 0).start()

    def finish(s, carry):
        y_copy(s, 2).wait()

        def out_rows(i, carry):
            r = pl.ds(pl.multiple_of(i * 16, 16), 16)
            g = slot_rows(s, own + i * 16, 16)
            block_o[g, :] = (middle[s, r, :] + total(s, 2, r) + db[...]).astype(BF)
            return carry

        lax.fori_loop(0, rows16, out_rows, 0)
        gather_copy(block_o, s, 2).start()
        y_copy(s, 3).wait()

        def rows(i, sums):
            r = pl.ds(pl.multiple_of(i * 16, 16), 16)
            g = slot_rows(s, own + i * 16, 16)
            n = total(s, 3, r)
            xn, scale = normalize(tok[g, :].astype(F32))
            ingrad_o[g, :] = (midgrad[s, r, :] + norm_back(n * g1[...], xn, scale)).astype(BF)
            return tuple(a + fold8(b) for a, b in zip(sums, (n * xn, n), strict=True))

        zero = jnp.zeros((8, width), F32)
        sums = lax.fori_loop(0, rows16, rows, (zero,) * 2)
        for i in range(2):
            acc[i] += sums[i]
        gather_copy(ingrad_o, s, 3).start()
        return carry

    lax.fori_loop(0, 2, finish, 0)

    for i in range(7):
        row = i if i < 6 else 8
        small_o[row : row + 1, :] = jnp.sum(acc[i], axis=0, keepdims=True)
    small_o[6:8, :] = jnp.zeros((2, width), F32)
    small_o[9:16, :] = jnp.zeros((7, width), F32)
    for i in range(2):
        small_o[9 + i : 10 + i, 0:third] = jnp.sum(accv[i], axis=0, keepdims=True)
    copy = remote(small_o.at[0:8], smc, s_send.at[0], s_recv.at[0], core_peer)
    copy.start()
    copy.wait()
    small_o[0:8, :] = small_o[0:8, :] + smc[...]
    for i in range(levels):
        copy = remote(small_o, smr.at[i], s_send.at[1 + i], s_recv.at[1 + i], dp_peer(i))
        copy.start()
        copy.wait()
        small_o[...] = small_o[...] + smr[i]

    def drain(s, carry):
        gather_copy(block_o, s, 2).wait()
        gather_copy(ingrad_o, s, 3).wait()
        return carry

    lax.fori_loop(0, 2, drain, 0)

    dp_add(1, 1)
    dp_last(0)
    dp_add(2, 0)
    dp_last(1)
    dp_gather(0, 2)
    dp_add(2, 1)
    dp_gather(1, 2)
    dp_gather(0, 1)
    dp_last(2)
    dp_gather(1, 1)
    dp_gather(0, 0)
    dp_gather(2, 2)
    dp_gather(1, 0)
    dp_gather(2, 1)
    dp_gather(2, 0)


def call_layer(n_dp, *operands):
    tok = operands[1]
    rows, width = tok.shape
    third = operands[4].shape[0]
    heads = third // HD
    levels = n_dp.bit_length() - 1
    extra = max(levels - 3, 1)
    vmem = pl.BlockSpec(memory_space=pltpu.VMEM)
    dma = pltpu.SemaphoreType.DMA
    return pl.pallas_call(
        functools.partial(layer_kernel, n_dp),
        out_shape=(
            jax.ShapeDtypeStruct((rows, width), BF),
            jax.ShapeDtypeStruct((rows, width), BF),
            jax.ShapeDtypeStruct((3, width, width), BF),
            jax.ShapeDtypeStruct((16, width), F32),
        ),
        in_specs=[pl.BlockSpec(memory_space=pltpu.SMEM)] + [vmem] * (len(operands) - 1),
        out_specs=(vmem,) * 4,
        scratch_shapes=[
            pltpu.VMEM((rows, width), BF),
            pltpu.VMEM((3, rows, third), BF),
            pltpu.VMEM((rows, third), BF),
            pltpu.VMEM((2 * heads, SLOT, SLOT), BF),
            pltpu.VMEM((rows, width), BF),
            pltpu.VMEM((rows, width), BF),
            pltpu.VMEM((rows, width), BF),
            pltpu.VMEM((2, HALF, width), F32),
            pltpu.VMEM((2, HALF, width), F32),
            pltpu.VMEM((rows, width), BF),
            pltpu.VMEM((rows, third), BF),
            pltpu.VMEM((3, rows, third), BF),
            pltpu.VMEM((2, SLOT, third), F32),
            pltpu.VMEM((HALF, width), F32),
            pltpu.VMEM((HALF, width), F32),
            pltpu.VMEM((7, 8, width), F32),
            pltpu.VMEM((2, 8, third), F32),
            pltpu.VMEM((HALF, width), BF),
            pltpu.VMEM((2, 4, HALF, width), BF),
            pltpu.VMEM((2, 4, HALF, width), BF),
            pltpu.VMEM((2, 4, HALF, width), BF),
            pltpu.VMEM((3, width, width), BF),
            pltpu.VMEM((3, width // 2, width), BF),
            pltpu.VMEM((3, width // 4, width), BF),
            pltpu.VMEM((3, width // 8, width), BF),
            pltpu.VMEM((extra, 3, width // 8, width), BF),
            pltpu.VMEM((8, width), F32),
            pltpu.VMEM((levels, 16, width), F32),
            dma((2, 4)),
            dma((2, 4)),
            dma((2, 4)),
            dma((2, 4)),
            dma((2, 4)),
            dma((2, 4)),
            dma((3, 6 + extra)),
            dma((3, 6 + extra)),
            dma((1 + levels,)),
            dma((1 + levels,)),
        ],
        compiler_params=pltpu.CompilerParams(
            collective_id=0, has_side_effects=True, vmem_limit_bytes=67043328
        ),
    )(*operands)


def group_lengths(image_group, image_length, group):
    in_group = image_group == group
    number = jnp.arange(image_group.shape[0], dtype=jnp.int32)
    first = jnp.min(jnp.where(in_group, number, image_group.shape[0]))
    length0 = jnp.sum(jnp.where(number == first, image_length, 0))
    return length0, jnp.sum(jnp.where(in_group, image_length, 0)) - length0


def to_slots(rows, length0, length1):
    row = jnp.arange(SLOT, dtype=jnp.int32)[:, None]
    small = rows[RES_SMALL : RES_SMALL + SLOT]
    large = jnp.pad(rows[RES_LARGE:], ((0, RES_LARGE + SLOT - rows.shape[0]), (0, 0)))
    zero = jnp.zeros((), rows.dtype)
    one = jnp.where(row < length0, rows[:SLOT], zero)
    two = jnp.where(row < length1, jnp.where(length0 == RES_SMALL, small, large), zero)
    return jnp.concatenate([one, two], axis=0)


def from_slots(slots, row_count, length0, length1):
    row = jnp.arange(row_count, dtype=jnp.int32)[:, None]
    small = jnp.concatenate([slots[:RES_SMALL], jnp.pad(slots[SLOT:], ((0, row_count - RES_SMALL - SLOT), (0, 0)))])
    large = jnp.concatenate([slots[:RES_LARGE], slots[SLOT : SLOT + row_count - RES_LARGE]])
    return jnp.where(row < length0 + length1, jnp.where(length0 == RES_SMALL, small, large), jnp.zeros((), slots.dtype))


def body(
    n_dp,
    tokens,
    cotangent,
    image_group,
    image_length,
    first_gain,
    first_shift,
    qkv_weight,
    qv_bias,
    out_weight,
    out_bias,
    second_gain,
    second_shift,
    up_weight,
    up_bias,
    down_weight,
    down_bias,
):
    third = out_weight.shape[0]
    width = tokens.shape[1]
    length0, length1 = group_lengths(image_group, image_length, lax.axis_index("dp"))
    block, ingrad, grads, small = call_layer(
        n_dp,
        jnp.stack([length0, length1]),
        to_slots(tokens, length0, length1),
        to_slots(cotangent, length0, length1),
        jnp.transpose(qkv_weight, (1, 0, 2)),
        out_weight,
        up_weight,
        down_weight,
        first_gain[None],
        first_shift[None],
        out_bias[None],
        second_gain[None],
        second_shift[None],
        down_bias[None],
        up_bias[None],
        qv_bias,
    )
    block_out = from_slots(block, tokens.shape[0], length0, length1)
    input_grad = from_slots(ingrad, tokens.shape[0], length0, length1).astype(F32)
    attn = grads[2].astype(F32)
    return (
        block_out,
        input_grad,
        small[0],
        small[1],
        jnp.transpose(attn[third:].reshape(3, third, width), (2, 0, 1)),
        small[9:11, :third],
        attn[:third],
        small[4],
        small[2],
        small[3],
        grads[1].astype(F32),
        small[8],
        grads[0].astype(F32),
        small[5],
    )


def solution(mesh):
    in_specs = (
        P("dp", None),
        P("dp", None),
        P(),
        P(),
        P(),
        P(),
        P(None, None, "tensor"),
        P(None, "tensor"),
        P("tensor", None),
        P(),
        P(),
        P(),
        P(None, "tensor"),
        P("tensor"),
        P("tensor", None),
        P(),
    )
    out_specs = (
        P("dp", None),
        P("dp", None),
        P(),
        P(),
        P(None, None, "tensor"),
        P(None, "tensor"),
        P("tensor", None),
        P(),
        P(),
        P(),
        P(None, "tensor"),
        P("tensor"),
        P("tensor", None),
        P(),
    )
    return jax.shard_map(
        functools.partial(body, mesh.shape["dp"]), mesh=mesh, in_specs=in_specs, out_specs=out_specs, check_vma=False
    )
```

time: 562 us -> 242 us (0.43); the launches traced: 553 us -> 241 us
  waiting for transfers between devices: 331 us -> 0 us
  Pallas kernels: 0 us -> 190 us
  matrix products: 69.9 us -> 0 us
  blocking collectives: 39.7 us -> 0 us
  local copies, waits for them, and re-layouts: 41.1 us -> 23.4 us
  other arithmetic: 41.8 us -> 24.7 us
  between operations: 18.7 us -> 2.73 us
  starting transfers between devices: 11.1 us -> 0 us
    psum x4 -> x0, waiting for transfers between devices: 331 us -> none  [the longest x1 191 us: body(): lax.psum((first_gain_grad, first_shift_grad, qkv_grad, qv_bias_grad, out_...]
    pallas_call x0 -> x1, Pallas kernels: none -> 190 us  [call_layer(): pl.pallas_call(functools.partial(layer_kernel, n_dp), out_shape=(jax.Shap...]
    dot_general x24 -> x0, matrix products: 69.9 us -> none  [the longest x4 13.3 us: outer_sum(): lax.dot_general(left_side, right_side, (((0,), (0,)), ((), ())), preferre...]
    psum x1 -> x0, blocking collectives: 39.7 us -> none  [body(): lax.psum((first_gain_grad, first_shift_grad, qkv_grad, qv_bias_grad, out_...]
    dynamic_update_slice x10 -> x0, local copies, waits for them, and re-layouts: 27.3 us -> none  [the longest x2 8.03 us: attention_forward(): lax.dynamic_update_slice_in_dim(attended_full, jnp.where(inside[:, None,...]
    reduce_sum x15 -> x1, other arithmetic: 24.3 us -> 1.96 us  [group_lengths(): length0 = jnp.sum(jnp.where(number == first, image_length, 0))]
    psum x4 -> x0, starting transfers between devices: 11.1 us -> none  [the longest x1 10.9 us: body(): lax.psum(normed_two_part.astype(jnp.bfloat16), 'tensor').astype(jnp.float32)]
    slice x4 -> x14, local copies, waits for them, and re-layouts: 1.16 us -> 11.4 us  [the longest x2 2.51 us: to_slots(): rows[RES_LARGE:]]
  transfers between devices with their start and end apart: 4 -> 0, of which waited for: 4 -> 0; matrix products, arithmetic and copies ran while one was open for 6% -> 0% of each run, Pallas kernels for 0% -> 0%
where the time goes in v1:
time: 242 us; the launch traced here: 241 us
  Pallas kernels  190 us (79%)
  other arithmetic  24.7 us (10%)
  local copies, waits for them, and re-layouts  23.4 us (10%)
  between operations  2.73 us (1%)
    pallas_call x1, Pallas kernels, call_layer(): pl.pallas_call(functools.partial(layer_kernel, n_dp), out_shape=(jax.Shap...  190 us
    convert_element_type x1, other arithmetic, body(): from_slots(ingrad, tokens.shape[0], length0, length1).astype(F32)  10.7 us

profile of v1, /device:TPU:0, one launch (start us, length us, event | category | flops | bytes accessed | tf_op | source)
XLA Modules:
  0.0 241.0 jit_solution(659379891963670292)
XLA Ops:
  0.6 1.3 fusion.10
  1.9 2.0 fusion.11
  5.8 0.0 copy-start.3
  5.9 1.4 pad_add_fusion.lens
  7.2 0.6 iota_compare_fusion.3
  7.9 1.2 iota_compare_fusion.1
  9.1 1.3 broadcast_in_dim.81.g1
  10.4 1.3 broadcast_in_dim.82.b1
  11.6 1.3 broadcast_in_dim.83.ob
  12.9 1.3 broadcast_in_dim.84.g2
  14.2 1.3 broadcast_in_dim.85.b2
  15.4 1.3 broadcast_in_dim.87.ub
  16.7 1.3 broadcast_in_dim.86.db
  18.0 1.4 slice.87
  19.4 0.0 copy-done.3
  19.4 0.0 copy-start.2
  19.4 1.1 slice.90
  20.5 2.3 copy.30
  22.8 0.0 copy-done.2
  22.8 2.8 %slice_select_fusion.1 = (bf16[608,768]{1,0:T(8,128)(2,1)S(1)}, bf16[608,768]{1,0:T(8,128)(2,1)S(1)}, bf16[608,768]{1,0:T(8,128)(2,1)S(1)}, bf16[608,768]{1,0:T(8,128)(2,1)S(1)}) fusion(bf16[1168,768]{1,0:T(8,128)(2,1)S(1)} %copy-done.2, pred[608]{0:T(1024)(128)(4,1)S(1)} %iota_compare_fusion.3, bf16[591,768]{1,0:T(8,128)(2,1)S(1)} %slice.87, pred[]{:T(512)S(6)} %eq.22, ...), kind=kLoop, calls=%fused_computation.18 | loop fusion | flops 2801664 | bytes 9287873 | tf_op jit(solution)/shard_map/jit(_where)/select_n | solution.py:585
  25.7 2.1 pad_maximum_fusion
  27.8 190.1 %shard_map.263 = (bf16[1216,768]{1,0:T(8,128)(2,1)}, bf16[1216,768]{1,0:T(8,128)(2,1)}, bf16[3,768,768]{2,1,0:T(8,128)(2,1)}, f32[16,768]{1,0:T(8,128)}) custom-call(s32[2]{0:T(128)} %pad_add_fusion.lens, bf16[1216,768]{1,0:T(8,128)(2,1)} %get-tuple-element.42.tok, bf16[1216,768]{1,0:T(8,128)(2,1)} %get-tuple-element.43.cot, bf16[3,768,192]{2,1,0:T(8,128)(2,1)} %bitcast.14, ...), custom_call_target="tpu_custom_call" | custom-call | tf_op jit(solution)/shard_map/pallas_call | solution.py:516
  217.9 0.0 copy-start
  217.9 1.4 slice.103
  219.3 1.6 slice_reduce_fusion
  220.9 1.0 slice.91
  221.9 1.0 slice.95
  222.9 0.0 copy-start.1
  222.9 1.4 slice.93
  224.3 0.0 copy-done
  224.3 0.1 slice.97
  224.4 0.3 copy-done.1
  224.7 0.1 slice.94
  224.7 0.1 slice.92
  224.8 0.0 copy-start.5
  224.8 0.1 slice.98
  224.9 0.1 slice.96
  225.0 0.5 copy-done.5
  225.5 0.0 copy-start.4
  225.5 10.7 %fusion.8 = (f32[1168,768]{1,0:T(8,128)}, bf16[1168,768]{1,0:T(8,128)(2,1)}) fusion(bf16[608,768]{1,0:T(8,128)(2,1)S(1)} %slice.96, bf16[197,768]{1,0:T(8,128)(2,1)S(1)} %slice.95, bf16[591,768]{1,0:T(8,128)(2,1)S(1)} %slice.98, bf16[577,768]{1,0:T(8,128)(2,1)S(1)} %slice.97, pred[1168]{0:T(1024)(128)(4,1)S(1)} %copy-done.5, pred[]{:T(512)S(6)} %eq.22, ...), kind=kLoop, calls=%fused_computation.11 | loop fusion | flops 21528576 | bytes 11444369 | tf_op jit(solution)/shard_map/convert_element_type | solution.py:638
  236.2 0.0 copy-done.4
  236.2 2.6 %bitcast_convert_fusion = (f32[768,768]{1,0:T(8,128)}, f32[768,768]{1,0:T(8,128)}, f32[1,768,768]{2,1,0:T(8,128)S(1)}) fusion(bf16[3,768,768]{2,1,0:T(8,128)(2,1)S(1)} %copy-done.4), kind=kLoop, calls=%fused_computation.12 | loop fusion | flops 1769472 | bytes 10616832 | tf_op jit(solution)/shard_map/convert_element_type | solution.py:653
  238.8 0.9 slice_bitcast_fusion
  239.7 1.3 slice.113
  (1 shorter events, 0.0 us)
Async XLA Ops:
  5.8 13.5 %copy-start.3 = (bf16[1168,768]{1,0:T(8,128)(2,1)S(1)}, bf16[1168,768]{1,0:T(8,128)(2,1)}, u32[]{:S(2)}) copy-start(bf16[1168,768]{1,0:T(8,128)(2,1)} %param.17) | copy-start | bytes 5382148
  19.4 3.5 %copy-start.2 = (bf16[1168,768]{1,0:T(8,128)(2,1)S(1)}, bf16[1168,768]{1,0:T(8,128)(2,1)}, u32[]{:S(2)}) copy-start(bf16[1168,768]{1,0:T(8,128)(2,1)} %param.16) | copy-start | bytes 5382148
  217.9 6.4 %copy-start = (bf16[1216,768]{1,0:T(8,128)(2,1)S(1)}, bf16[1216,768]{1,0:T(8,128)(2,1)}, u32[]{:S(2)}) copy-start(bf16[1216,768]{1,0:T(8,128)(2,1)} %get-tuple-element.19) | copy-start | bytes 5603332
  222.9 1.8 copy-start.1
  224.8 0.7 copy-start.5
  225.5 10.7 %copy-start.4 = (bf16[3,768,768]{2,1,0:T(8,128)(2,1)S(1)}, bf16[3,768,768]{2,1,0:T(8,128)(2,1)}, u32[]{:S(2)}) copy-start(bf16[3,768,768]{2,1,0:T(8,128)(2,1)} %get-tuple-element.21) | copy-start | bytes 10616836

commit v2 on v1

v2 whole, which is shorter than its diff:
```python
import functools

import jax
import jax.numpy as jnp
from jax import lax
from jax.experimental import pallas as pl
from jax.experimental.pallas import tpu as pltpu
from jax.sharding import PartitionSpec as P

HD = 64
RES_SMALL = 197
RES_LARGE = 577
SMALL_START = RES_SMALL // 16 * 16
LARGE_START = RES_LARGE // 16 * 16
SLOT = 608
HALF = 304
EPS = 1e-06
MASKED = -1e30
BF = jnp.bfloat16
F32 = jnp.float32
MESH = pl.DeviceIdType.MESH


def dot_nn(a, b):
    return lax.dot_general(a, b, (((1,), (0,)), ((), ())), preferred_element_type=F32)


def dot_nt(a, b):
    return lax.dot_general(a, b, (((1,), (1,)), ((), ())), preferred_element_type=F32)


def dot_tn(a, b):
    return lax.dot_general(a, b, (((0,), (0,)), ((), ())), preferred_element_type=F32)


def normalize(x):
    mean = jnp.mean(x, axis=-1, keepdims=True)
    centered = x - mean
    var = jnp.mean(centered * centered, axis=-1, keepdims=True)
    scale = lax.rsqrt(var + EPS)
    return centered * scale, scale


def norm_back(u, xn, scale):
    return scale * (
        u
        - jnp.mean(u, axis=-1, keepdims=True)
        - xn * jnp.mean(u * xn, axis=-1, keepdims=True)
    )


def fold8(x):
    return jnp.sum(x.reshape(x.shape[0] // 8, 8, x.shape[1]), axis=0)


def flip(index, stride):
    return index + stride - 2 * stride * ((index // stride) % 2)


def row_loop(count, size, unroll, step, init):
    block = size * unroll

    def several(i, carry):
        for j in range(unroll):
            carry = step(pl.multiple_of(i * block + j * size, 16), carry)
        return carry

    carry = lax.fori_loop(0, count // block, several, init)
    for off in range(count // block * block, count, size):
        carry = step(off, carry)
    return carry


def layer_kernel(
    n_dp,
    group,
    lengths,
    tok_h,
    cot_h,
    wqkv_h,
    wout_h,
    wup_h,
    wdown_h,
    g1,
    b1,
    ob,
    g2,
    b2,
    db,
    ub,
    qvb,
    block_h,
    ingrad_h,
    grads_h,
    small_o,
    tok,
    cot,
    wqkv,
    wout,
    wup,
    wdown,
    vec,
    normed,
    qkv,
    att,
    attc,
    attf,
    probs,
    hidden,
    pregrad,
    middle,
    midgrad,
    mg,
    agrad,
    dqkv,
    dacc,
    tmp_a,
    tmp_b,
    acc,
    accv,
    csend,
    crecv,
    ysend,
    yrecv,
    gbuf,
    obuf,
    rx,
    block,
    ingrad,
    smc,
    smr,
    l_sem,
    w_send,
    w_recv,
    a_send,
    a_recv,
    c_send,
    c_recv,
    y_send,
    y_recv,
    g_send,
    g_recv,
    d_send,
    d_recv,
    s_send,
    s_recv,
    *more,
):
    rs, normed2 = more[:12], (more[12:14], more[14:16])
    levels = n_dp.bit_length() - 1
    d = lax.axis_index("dp")
    t = lax.axis_index("tensor")
    core = t % 2
    side = t // 2
    core_peer = (d, flip(t, 1))
    y_peer = (d, flip(t, 2))
    rows, width = tok_h.shape
    third = wout_h.shape[0]
    heads = third // HD

    def dp_peer(level):
        return (flip(d, 2**level), t)

    def local(i, src, dst):
        return pltpu.make_async_copy(src, dst, l_sem.at[i])

    my_quarter = pl.ds(pl.multiple_of(t * third, 16), third)
    its_quarter = pl.ds(pl.multiple_of(flip(t, 2) * third, 16), third)
    loads = [
        local(0, tok_h, tok.at[0:rows]),
        local(1, wqkv_h, wqkv),
        local(2, wout_h, wout.at[my_quarter]),
        local(3, cot_h, hidden.at[0:rows]),
        local(4, wup_h, wup),
        local(5, wdown_h, wdown),
    ]
    for copy in loads:
        copy.start()
    bar = pltpu.get_barrier_semaphore()
    peers = [core_peer, y_peer] + [dp_peer(i) for i in range(levels)]
    for peer in peers:
        pl.semaphore_signal(bar, inc=1, device_id=peer, device_id_type=MESH)

    def look(i, found):
        count, first, second = found
        here = group[i] == d
        first = jnp.where(here & (count == 0), lengths[i], first)
        second = jnp.where(here & (count == 1), lengths[i], second)
        return count + here.astype(jnp.int32), first, second

    zero = jnp.int32(0)
    _, first_len, second_len = lax.fori_loop(0, group.shape[0], look, (zero, zero, zero))
    first_small = first_len == RES_SMALL
    second_skip = jnp.where(first_small, RES_SMALL % 16, RES_LARGE % 16)

    def group_rows(ref, s, off, size):
        small = ref[pl.ds(pl.multiple_of(s * SMALL_START + off, 16), size), :].astype(F32)
        large = ref[pl.ds(pl.multiple_of(s * LARGE_START + off, 16), size), :].astype(F32)
        return jnp.where(first_small, small, large)

    def inside(s, index):
        low = s * second_skip
        return (index >= low) & (index < low + jnp.where(s == 0, first_len, second_len))

    for i, ref in enumerate((g1, b1, ob, g2, b2, db, ub)):
        vec[i : i + 1, :] = ref[...][None, :]
    gain1, shift1, bias_out, gain2, shift2, bias_down, bias_up = (vec.at[i : i + 1] for i in range(7))
    acc[...] = jnp.zeros_like(acc)
    accv[...] = jnp.zeros_like(accv)
    tok[rows:, :] = jnp.zeros((tok.shape[0] - rows, width), BF)

    own, other = 0, HALF
    half_start = (core * HALF, (1 - core) * HALF)
    lane_head = lax.broadcasted_iota(jnp.int32, (1, third), 1) // HD
    zero8 = jnp.zeros((8, width), F32)

    def slot_rows(s, off, size):
        return pl.ds(pl.multiple_of(s * SLOT + off, 16), size)

    def remote(src, dst, send, recv, peer):
        return pltpu.make_async_remote_copy(
            src_ref=src, dst_ref=dst, send_sem=send, recv_sem=recv, device_id=peer, device_id_type=MESH
        )

    def c_copy(s, k):
        return remote(csend, crecv.at[s, k], c_send.at[s, k], c_recv.at[s, k], core_peer)

    def y_copy(s, k):
        return remote(ysend.at[s, k], yrecv.at[s, k], y_send.at[s, k], y_recv.at[s, k], y_peer)

    def norm_copy(s):
        return remote(normed2[s][0], normed2[s][1], g_send.at[s, 0], g_recv.at[s, 0], core_peer)

    def half_copy(ref, s, k):
        mine, its = slot_rows(s, own, HALF), slot_rows(s, other, HALF)
        return remote(ref.at[mine], ref.at[its], g_send.at[s, k], g_recv.at[s, k], core_peer)

    def gather_copy(ref, s, k):
        region = slot_rows(s, half_start[0], HALF)
        return remote(ref.at[region], ref.at[region], g_send.at[s, k], g_recv.at[s, k], core_peer)

    def stage(s, k, part):
        csend[...] = part(other).astype(BF)
        copy = c_copy(s, k)
        copy.start()
        tmp_a[...] = part(own)
        copy.wait()

        def add(off, carry):
            r = pl.ds(off, 16)
            ysend[s, k, r, :] = (tmp_a[r, :] + crecv[s, k, r, :].astype(F32)).astype(BF)
            return carry

        row_loop(HALF, 16, 6, add, 0)
        y_copy(s, k).start()

    def total(s, k, r):
        return ysend[s, k, r, :].astype(F32) + yrecv[s, k, r, :].astype(F32)

    units = [
        (0, width, (0, 1, 2)),
        (width, width, (1, 0, 2)),
        (2 * width, 2 * third, (0, 1, 2)),
        (2 * width + 2 * third, 2 * third, (1, 0, 2)),
    ]

    def bit(level):
        return (d // 2**level) % 2

    def base(u, depth):
        row0, size, order = units[u]
        for i in range(depth):
            row0 = row0 + bit(order[i]) * (size >> (i + 1))
        return row0

    def dp_rs(u, i):
        _, size, order = units[u]
        part = size >> (i + 1)
        src = pl.ds(pl.multiple_of(base(u, i) + (1 - bit(order[i])) * part, 16), part)
        return remote(gbuf.at[src], rs[3 * u + i], d_send.at[u, i], d_recv.at[u, i], dp_peer(order[i]))

    def dp_add(u, i):
        _, size, _ = units[u]
        dp_rs(u, i).wait()
        start = base(u, i + 1)
        out = obuf if i == 2 else gbuf

        def add(off, carry):
            r = pl.ds(pl.multiple_of(start + off, 16), 16)
            out[r, :] = (gbuf[r, :].astype(F32) + rs[3 * u + i][pl.ds(off, 16), :].astype(F32)).astype(BF)
            return carry

        row_loop(size >> (i + 1), 16, 3, add, 0)

    def dp_extra(u):
        row0, size, _ = units[u]
        mine = pl.ds(pl.multiple_of(base(u, 3), 16), size >> 3)
        spot = pl.ds(row0 >> 3, size >> 3)
        for e in range(levels - 3):
            copy = remote(obuf.at[mine], rx.at[e, spot], d_send.at[u, 6 + e], d_recv.at[u, 6 + e], dp_peer(3 + e))
            copy.start()
            copy.wait()
            obuf[mine, :] = (obuf[mine, :].astype(F32) + rx[e, spot, :].astype(F32)).astype(BF)

    def dp_ag(u, i):
        _, size, order = units[u]
        region = pl.ds(pl.multiple_of(base(u, i + 1), 16), size >> (i + 1))
        return remote(obuf.at[region], obuf.at[region], d_send.at[u, 3 + i], d_recv.at[u, 3 + i], dp_peer(order[i]))

    def dp_out(u):
        row0, size, _ = units[u]
        return local(6 + u, obuf.at[row0 : row0 + size], grads_h.at[row0 : row0 + size])

    def advance(u, k):
        if k < 2:
            dp_add(u, k)
            dp_rs(u, k + 1).start()
        elif k == 2:
            dp_add(u, 2)
            dp_extra(u)
            dp_ag(u, 2).start()
        else:
            dp_ag(u, 5 - k).wait()
            if k < 5:
                dp_ag(u, 4 - k).start()
            else:
                dp_out(u).start()

    def serve(*steps):
        for u, k in steps:
            advance(u, k)

    def norm_rows(s):
        for half, start in enumerate(half_start):

            def step(off, carry):
                xn, _ = normalize(group_rows(tok, s, start + off, 16))
                normed[slot_rows(s, half * HALF + off, 16), :] = (xn * gain1[...] + shift1[...]).astype(BF)
                return carry

            row_loop(HALF, 16, 6, step, 0)

    def mask_rows(s):
        for half, start in enumerate(half_start):

            def step(off, carry):
                ok = inside(s, lax.broadcasted_iota(jnp.int32, (16, 1), 0) + (start + off))
                value = group_rows(hidden, s, start + off, 16)
                cot[slot_rows(s, half * HALF + off, 16), :] = jnp.where(ok, value, 0.0).astype(BF)
                return carry

            row_loop(HALF, 16, 6, step, 0)

    loads[0].wait()
    norm_rows(0)
    pl.semaphore_wait(bar, len(peers))
    loads[2].wait()
    w_own = [
        remote(wout.at[my_quarter], wout.at[my_quarter], w_send.at[0], w_recv.at[0], core_peer),
        remote(wout.at[my_quarter], wout.at[my_quarter], w_send.at[1], w_recv.at[1], y_peer),
    ]
    w_pass = remote(wout.at[its_quarter], wout.at[its_quarter], w_send.at[2], w_recv.at[2], core_peer)
    for copy in w_own:
        copy.start()
    loads[1].wait()
    norm_rows(1)

    def a_swap(s):
        return remote(att.at[slot_rows(s, other, HALF)], attc.at[s], a_send.at[s, 0], a_recv.at[s, 0], core_peer)

    def a_copy(s):
        return remote(attf.at[s, side], attf.at[s, side], a_send.at[s, 1], a_recv.at[s, 1], y_peer)

    def forward_attention(s, carry):
        def project(i, carry):
            r = slot_rows(s, i * HALF, HALF)
            x = normed[r, :]
            qkv[0, r, :] = (dot_nt(x, wqkv[0]) + qvb[0:1, :]).astype(BF)
            qkv[1, r, :] = dot_nt(x, wqkv[1]).astype(BF)
            qkv[2, r, :] = (dot_nt(x, wqkv[2]) + qvb[1:2, :]).astype(BF)
            return carry

        lax.fori_loop(0, 2, project, 0)
        whole = slot_rows(s, 0, SLOT)
        key = lax.broadcasted_iota(jnp.int32, (1, SLOT), 1)
        key = key + jnp.where(key < HALF, half_start[0], half_start[1] - HALF)
        key_bias = jnp.where(inside(s, key), 0.0, MASKED)

        def attend(i, carry):
            r = slot_rows(s, i * HALF, HALF)
            for h in range(heads):
                q = jnp.where(lane_head == h, qkv[0, r, :] * HD**-0.5, 0.0).astype(BF)
                scores = dot_nt(q, qkv[1, whole, :]) + key_bias
                exps = jnp.exp(scores - jnp.max(scores, axis=-1, keepdims=True))
                weights = (exps * (1.0 / jnp.sum(exps, axis=-1, keepdims=True))).astype(BF)
                probs[s * heads + h, pl.ds(pl.multiple_of(i * HALF, 16), HALF), :] = weights
                part = dot_nn(weights, qkv[2, whole, :])
                result = part if h == 0 else jnp.where(lane_head == h, part, result)
            att[r, :] = result.astype(BF)
            return carry

        lax.fori_loop(0, 2, attend, 0)
        a_swap(s).start()
        a_swap(s).wait()
        mine, its = att[slot_rows(s, own, HALF), :], attc[s]
        left = jnp.where(core == 0, mine, its)
        right = jnp.where(core == 0, its, mine)
        attf[s, side] = jnp.concatenate([left, right], axis=1)
        a_copy(s).start()
        return carry

    lax.fori_loop(0, 2, forward_attention, 0)
    w_own[1].wait()
    w_pass.start()
    loads[3].wait()
    mask_rows(0)
    mask_rows(1)
    w_own[0].wait()
    w_pass.wait()
    loads[4].wait()
    loads[5].wait()

    def second_norm(s):
        a_copy(s).wait()
        tmp_a[...] = dot_nn(jnp.concatenate([attf[s, 0], attf[s, 1]], axis=1), wout[...])

        def step(off, carry):
            r = pl.ds(off, 16)
            m = tmp_a[r, :] + group_rows(tok, s, half_start[0] + off, 16) + bias_out[...]
            middle[s, r, :] = m
            xn, _ = normalize(m)
            normed2[s][0][r, :] = (xn * gain2[...] + shift2[...]).astype(BF)
            return carry

        row_loop(HALF, 16, 6, step, 0)
        norm_copy(s).start()

    def feed_forward(s):
        second_norm(s)

        def half(start):
            r = slot_rows(s, start, HALF)
            tmp_a[...] = dot_nn(normed2[s][start // HALF][...], wup[...])
            tmp_b[...] = dot_nt(cot[r, :], wdown[...])

            def step(off, sums):
                rr = pl.ds(off, 16)
                g = slot_rows(s, start + off, 16)
                x = tmp_a[rr, :] + bias_up[...]
                phi = 0.5 + 0.5 * lax.erf(x * 0.7071067811865476)
                hidden[g, :] = (x * phi).astype(BF)
                slope = phi + x * (jnp.exp(x * x * -0.5) * 0.3989422804014327)
                low = (tmp_b[rr, :] * slope).astype(BF)
                pregrad[g, :] = low
                return sums + fold8(low.astype(F32))

            acc[6] += row_loop(HALF, 16, 1, step, zero8)

        half(own)
        norm_copy(s).wait()
        half(other)
        stage(s, 0, lambda off: dot_nt(pregrad[slot_rows(s, off, HALF), :], wup[...]))

    feed_forward(0)
    feed_forward(1)

    def weight_grad(u, left, right):
        row0, size, order = units[u]
        for mine in (0, 1):
            off = (bit(order[0]) if mine else 1 - bit(order[0])) * (size // 2)

            columns = left(pl.ds(pl.multiple_of(off, 128), size // 2))
            gbuf[pl.ds(pl.multiple_of(row0 + off, 16), size // 2), :] = dot_tn(columns, right[...]).astype(BF)
            if not mine:
                dp_rs(u, 0).start()

    def norm_columns(columns):
        return jnp.concatenate([ref[:, columns] for refs in normed2 for ref in refs], axis=0)

    weight_grad(0, lambda columns: hidden[:, columns], cot)
    weight_grad(1, norm_columns, pregrad)

    def feed_forward_out(s, carry):
        stage(s, 1, lambda off: dot_nn(hidden[slot_rows(s, off, HALF), :], wdown[...]))
        return carry

    lax.fori_loop(0, 2, feed_forward_out, 0)

    def second_back(s):
        y_copy(s, 0).wait()

        def step(off, sums):
            r = pl.ds(off, 16)
            g = slot_rows(s, own + off, 16)
            n = total(s, 0, r)
            xn, scale = normalize(middle[s, r, :])
            og = cot[g, :].astype(F32)
            m = og + norm_back(n * gain2[...], xn, scale)
            midgrad[s, r, :] = m
            mg[g, :] = m.astype(BF)
            return tuple(a + fold8(b) for a, b in zip(sums, (n * xn, n, m, og), strict=True))

        sums = row_loop(HALF, 16, 3, step, (zero8,) * 4)
        for i in range(4):
            acc[2 + i] += sums[i]
        half_copy(mg, s, 1).start()

    def attention_back(s, services):
        second_back(s)
        half_copy(mg, s, 1).wait()
        whole = slot_rows(s, 0, SLOT)
        agrad[whole, :] = dot_nt(mg[whole, :], wout[my_quarter, :]).astype(BF)
        dacc[...] = jnp.zeros_like(dacc)

        def chunk(i):
            r = slot_rows(s, i * HALF, HALF)
            for h in range(heads):
                mask = lane_head == h
                do = agrad[r, :]
                w = probs[s * heads + h, pl.ds(pl.multiple_of(i * HALF, 16), HALF), :]
                prob_grad = dot_nt(jnp.where(mask, do, 0.0).astype(BF), qkv[2, whole, :])
                p = w.astype(F32)
                inner = jnp.sum(p * prob_grad, axis=-1, keepdims=True)
                score_grad = (p * (prob_grad - inner)).astype(BF)
                part = dot_nn(score_grad, qkv[1, whole, :])
                dq = part if h == 0 else jnp.where(mask, part, dq)
                dacc[0] += jnp.where(mask, dot_tn(score_grad, qkv[0, r, :]), 0.0)
                dacc[1] += jnp.where(mask, dot_tn(w, do), 0.0)
            low = (dq * HD**-0.5).astype(BF)
            dqkv[0, r, :] = low
            accv[0] += fold8(low.astype(F32))

            serve(*services[i])

        chunk(0)
        chunk(1)
        dqkv[1, whole, :] = (dacc[0] * HD**-0.5).astype(BF)
        low = dacc[1].astype(BF)
        dqkv[2, whole, :] = low
        accv[1] += fold8(low.astype(F32))

        def part(off):
            r = slot_rows(s, off, HALF)
            return dot_nn(dqkv[0, r, :], wqkv[0]) + dot_nn(dqkv[1, r, :], wqkv[1]) + dot_nn(dqkv[2, r, :], wqkv[2])

        stage(s, 2, part)

    attention_back(0, (((0, 0),), ((1, 0),)))
    attention_back(1, (((0, 1), (1, 1)), ((0, 2), (1, 2))))

    low0 = 2 * width
    gbuf[low0 : low0 + third, :] = dot_tn(att[...], mg[...]).astype(BF)
    gbuf[low0 + third : low0 + 2 * third, :] = dot_tn(dqkv[0], normed[...]).astype(BF)
    dp_rs(2, 0).start()
    gbuf[low0 + 2 * third : low0 + 3 * third, :] = dot_tn(dqkv[1], normed[...]).astype(BF)
    gbuf[low0 + 3 * third : low0 + 4 * third, :] = dot_tn(dqkv[2], normed[...]).astype(BF)
    dp_rs(3, 0).start()
    serve((0, 3), (1, 3))

    def finish_block(s):
        y_copy(s, 1).wait()

        def step(off, carry):
            r = pl.ds(off, 16)
            block[slot_rows(s, half_start[0] + off, 16), :] = (middle[s, r, :] + total(s, 1, r) + bias_down[...]).astype(BF)
            return carry

        row_loop(HALF, 16, 6, step, 0)
        gather_copy(block, s, 2).start()

    def finish_grad(s):
        y_copy(s, 2).wait()

        def step(off, sums):
            r = pl.ds(off, 16)
            n = total(s, 2, r)
            xn, scale = normalize(group_rows(tok, s, half_start[0] + off, 16))
            ingrad[slot_rows(s, half_start[0] + off, 16), :] = (midgrad[s, r, :] + norm_back(n * gain1[...], xn, scale)).astype(BF)
            return tuple(a + fold8(b) for a, b in zip(sums, (n * xn, n), strict=True))

        sums = row_loop(HALF, 16, 4, step, (zero8,) * 2)
        for i in range(2):
            acc[i] += sums[i]
        gather_copy(ingrad, s, 3).start()

    def assemble(ref):
        def step(off, carry):
            index = lax.broadcasted_iota(jnp.int32, (16, 1), 0) + off

            def two_from(start):
                source = jnp.clip(off - start, 0, SLOT - 16) + SLOT
                return ref[pl.ds(pl.multiple_of(source, 16), 16), :].astype(F32)

            two = jnp.where(first_small, two_from(SMALL_START), two_from(LARGE_START))
            low = jnp.minimum(off, SLOT - 16)
            one = ref[pl.ds(pl.multiple_of(low, 16), 16), :].astype(F32)
            both = jnp.where(index < first_len, one, two)
            ref[pl.ds(off, 16), :] = jnp.where(index < first_len + second_len, both, 0.0).astype(BF)
            return carry

        row_loop(rows, 16, 1, step, 0)

    serve((2, 0), (3, 0))
    finish_block(0)
    serve((0, 4), (1, 4), (2, 1), (3, 1))
    finish_block(1)
    serve((0, 5), (1, 5), (2, 2), (3, 2))
    for s in (0, 1):
        gather_copy(block, s, 2).wait()
    assemble(block)
    out_block = local(10, block.at[0:rows], block_h)
    out_block.start()
    serve((2, 3), (3, 3))
    finish_grad(0)
    serve((2, 4), (3, 4))
    finish_grad(1)

    for i in range(7):
        row = i if i < 6 else 8
        small_o[row : row + 1, :] = jnp.sum(acc[i], axis=0, keepdims=True)
    small_o[6:8, :] = jnp.zeros((2, width), F32)
    small_o[9:16, :] = jnp.zeros((7, width), F32)
    for i in range(2):
        small_o[9 + i : 10 + i, 0:third] = jnp.sum(accv[i], axis=0, keepdims=True)
    copy = remote(small_o.at[0:8], smc, s_send.at[0], s_recv.at[0], core_peer)
    copy.start()
    copy.wait()
    small_o[0:8, :] = small_o[0:8, :] + smc[...]
    copy = remote(small_o, smr.at[0], s_send.at[1], s_recv.at[1], dp_peer(0))
    copy.start()
    for s in (0, 1):
        gather_copy(ingrad, s, 3).wait()
    assemble(ingrad)
    out_grad = local(11, ingrad.at[0:rows], ingrad_h)
    out_grad.start()
    for i in range(levels):
        if i:
            copy = remote(small_o, smr.at[i], s_send.at[1 + i], s_recv.at[1 + i], dp_peer(i))
            copy.start()
        copy.wait()
        small_o[...] = small_o[...] + smr[i]
    serve((2, 5), (3, 5))
    out_block.wait()
    out_grad.wait()
    for u in range(4):
        dp_out(u).wait()


def unpack_kernel(block, ingrad, down, up, out, qkv, small, *outs):
    outs[0][...] = block[...]
    outs[1][...] = ingrad[...].astype(F32)
    outs[2][...] = down[...].astype(F32)
    outs[3][...] = up[...].astype(F32)
    outs[4][...] = out[...].astype(F32)
    outs[5][...] = qkv[...].astype(F32)

    @pl.when(pl.program_id(0) == 0)
    def _():
        for i, row in enumerate((0, 1, 2, 3, 4, 5, 8)):
            outs[6 + i][...] = small[row]
        outs[13][...] = small[9:11, 0 : outs[13].shape[1]]


def call_unpack(block, ingrad, grads, small, third):
    rows, width = block.shape
    steps = 6
    row_block = -(-rows // (16 * steps)) * 16

    def part(size, start):
        return pl.BlockSpec((size, width), lambda i: (start // size + i, 0))

    def whole(shape):
        return pl.BlockSpec(shape, lambda i: (0,) * len(shape))

    big, mid, low = width // steps, 3 * third // steps, third // steps
    shapes = [
        ((rows, width), BF, part(row_block, 0)),
        ((rows, width), F32, part(row_block, 0)),
        ((width, width), F32, part(big, 0)),
        ((width, width), F32, part(big, 0)),
        ((third, width), F32, part(low, 0)),
        ((3 * third, width), F32, part(mid, 0)),
    ]
    shapes += [((width,), F32, whole((width,)))] * 7 + [((2, third), F32, whole((2, third)))]
    return pl.pallas_call(
        unpack_kernel,
        grid=(steps,),
        out_shape=[jax.ShapeDtypeStruct(shape, kind) for shape, kind, _ in shapes],
        in_specs=[
            part(row_block, 0),
            part(row_block, 0),
            part(big, 0),
            part(big, width),
            part(low, 2 * width),
            part(mid, 2 * width + third),
            whole(small.shape),
        ],
        out_specs=[spec for _, _, spec in shapes],
    )(block, ingrad, grads, grads, grads, grads, small)


def call_layer(n_dp, *operands):
    rows, width = operands[2].shape
    third = operands[5].shape[0]
    heads = third // HD
    levels = n_dp.bit_length() - 1
    extra = max(levels - 3, 1)
    slots = 2 * SLOT
    grad_rows = 2 * width + 4 * third
    vmem = pl.BlockSpec(memory_space=pltpu.VMEM)
    smem = pl.BlockSpec(memory_space=pltpu.SMEM)
    hbm = pl.BlockSpec(memory_space=pl.ANY)
    dma = pltpu.SemaphoreType.DMA
    return pl.pallas_call(
        functools.partial(layer_kernel, n_dp),
        out_shape=(
            jax.ShapeDtypeStruct((rows, width), BF),
            jax.ShapeDtypeStruct((rows, width), BF),
            jax.ShapeDtypeStruct((grad_rows, width), BF),
            jax.ShapeDtypeStruct((16, width), F32),
        ),
        in_specs=[smem] * 2 + [hbm] * 6 + [vmem] * 8,
        out_specs=(hbm, hbm, hbm, vmem),
        scratch_shapes=[
            pltpu.VMEM((rows + 16, width), BF),
            pltpu.VMEM((slots, width), BF),
            pltpu.VMEM((3, third, width), BF),
            pltpu.VMEM((4 * third, width), BF),
            pltpu.VMEM((width, width), BF),
            pltpu.VMEM((width, width), BF),
            pltpu.VMEM((8, width), F32),
            pltpu.VMEM((slots, width), BF),
            pltpu.VMEM((3, slots, third), BF),
            pltpu.VMEM((slots, third), BF),
            pltpu.VMEM((2, HALF, third), BF),
            pltpu.VMEM((2, 2, HALF, 2 * third), BF),
            pltpu.VMEM((2 * heads, SLOT, SLOT), BF),
            pltpu.VMEM((slots, width), BF),
            pltpu.VMEM((slots, width), BF),
            pltpu.VMEM((2, HALF, width), F32),
            pltpu.VMEM((2, HALF, width), F32),
            pltpu.VMEM((slots, width), BF),
            pltpu.VMEM((slots, third), BF),
            pltpu.VMEM((3, slots, third), BF),
            pltpu.VMEM((2, SLOT, third), F32),
            pltpu.VMEM((HALF, width), F32),
            pltpu.VMEM((HALF, width), F32),
            pltpu.VMEM((7, 8, width), F32),
            pltpu.VMEM((2, 8, third), F32),
            pltpu.VMEM((HALF, width), BF),
            pltpu.VMEM((2, 3, HALF, width), BF),
            pltpu.VMEM((2, 3, HALF, width), BF),
            pltpu.VMEM((2, 3, HALF, width), BF),
            pltpu.VMEM((grad_rows, width), BF),
            pltpu.VMEM((grad_rows, width), BF),
            pltpu.VMEM((extra, grad_rows // 8, width), BF),
            pltpu.VMEM((slots, width), BF),
            pltpu.VMEM((slots, width), BF),
            pltpu.VMEM((8, width), F32),
            pltpu.VMEM((levels, 16, width), F32),
            dma((12,)),
            dma((3,)),
            dma((3,)),
            dma((2, 2)),
            dma((2, 2)),
            dma((2, 3)),
            dma((2, 3)),
            dma((2, 3)),
            dma((2, 3)),
            dma((2, 4)),
            dma((2, 4)),
            dma((4, 6 + extra)),
            dma((4, 6 + extra)),
            dma((1 + levels,)),
            dma((1 + levels,)),
        ]
        + [pltpu.VMEM((size >> (i + 1), width), BF) for size in (width, width, 2 * third, 2 * third) for i in range(3)]
        + [pltpu.VMEM((HALF, width), BF)] * 4,
        compiler_params=pltpu.CompilerParams(
            collective_id=0, has_side_effects=True, vmem_limit_bytes=67043328
        ),
    )(*operands)


def body(
    n_dp,
    tokens,
    cotangent,
    image_group,
    image_length,
    first_gain,
    first_shift,
    qkv_weight,
    qv_bias,
    out_weight,
    out_bias,
    second_gain,
    second_shift,
    up_weight,
    up_bias,
    down_weight,
    down_bias,
):
    third = out_weight.shape[0]
    width = tokens.shape[1]
    block, ingrad, grads, small = call_layer(
        n_dp,
        image_group,
        image_length,
        tokens,
        cotangent,
        jnp.transpose(qkv_weight, (1, 2, 0)),
        out_weight,
        up_weight,
        down_weight,
        first_gain,
        first_shift,
        out_bias,
        second_gain,
        second_shift,
        down_bias,
        up_bias,
        qv_bias,
    )
    outs = call_unpack(block, ingrad, grads, small, third)
    block_out, input_grad, down_grad, up_grad, out_grad, qkv_grad = outs[:6]
    g1, b1, g2, b2, out_bias_grad, down_bias_grad, up_bias_grad, qv_bias_grad = outs[6:]
    return (
        block_out,
        input_grad,
        g1,
        b1,
        jnp.transpose(qkv_grad.reshape(3, third, width), (2, 0, 1)),
        qv_bias_grad,
        out_grad,
        out_bias_grad,
        g2,
        b2,
        up_grad,
        up_bias_grad,
        down_grad,
        down_bias_grad,
    )


def solution(mesh):
    in_specs = (
        P("dp", None),
        P("dp", None),
        P(),
        P(),
        P(),
        P(),
        P(None, None, "tensor"),
        P(None, "tensor"),
        P("tensor", None),
        P(),
        P(),
        P(),
        P(None, "tensor"),
        P("tensor"),
        P("tensor", None),
        P(),
    )
    out_specs = (
        P("dp", None),
        P("dp", None),
        P(),
        P(),
        P(None, None, "tensor"),
        P(None, "tensor"),
        P("tensor", None),
        P(),
        P(),
        P(),
        P(None, "tensor"),
        P("tensor"),
        P("tensor", None),
        P(),
    )
    return jax.shard_map(
        functools.partial(body, mesh.shape["dp"]), mesh=mesh, in_specs=in_specs, out_specs=out_specs, check_vma=False
    )
```

time: 242 us -> 165 us (0.68)
  Pallas kernels: 190 us -> 164 us
  other arithmetic: 24.7 us -> 0 us
  local copies, waits for them, and re-layouts: 23.4 us -> 0 us
    pallas_call x1, Pallas kernels: 190 us -> 155 us  [call_layer(): pl.pallas_call(functools.partial(layer_kernel, n_dp), out_shape=(jax.Shap...]
    convert_element_type x2 -> x0, other arithmetic: 13.3 us -> none  [the longest x1 10.7 us: body(): from_slots(ingrad, tokens.shape[0], length0, length1).astype(F32)]
    slice x14 -> x0, local copies, waits for them, and re-layouts: 11.4 us -> none  [the longest x2 2.51 us: to_slots(): rows[RES_LARGE:]]
    broadcast_in_dim x7 -> x0, local copies, waits for them, and re-layouts: 8.86 us -> none  [the longest x1 1.27 us: body(): first_shift[None]]
    pallas_call x0 -> x1, Pallas kernels: none -> 8.44 us  [call_unpack(): pl.pallas_call(unpack_kernel, grid=(steps,), out_shape=[jax.ShapeDtypeStr...]
    unnamed x13 -> x0, local copies, waits for them, and re-layouts: 3.2 us -> none
    select_n x1 -> x0, other arithmetic: 2.84 us -> none  [to_slots(): one = jnp.where(row < length0, rows[:SLOT], zero)]
where the time goes in v2:
time: 165 us
  Pallas kernels  164 us (99%)
    pallas_call x1, Pallas kernels, call_layer(): pl.pallas_call(functools.partial(layer_kernel, n_dp), out_shape=(jax.Shap...  155 us
    pallas_call x1, Pallas kernels, call_unpack(): pl.pallas_call(unpack_kernel, grid=(steps,), out_shape=[jax.ShapeDtypeStr...  8.44 us

profile of v2, /device:TPU:0, one launch (start us, length us, event | category | flops | bytes accessed | tf_op | source)
XLA Modules:
  0.0 164.7 jit_solution(2472059835982773695)
XLA Ops:
  0.7 155.5 %shard_map.263 = (bf16[1168,768]{1,0:T(8,128)(2,1)}, bf16[1168,768]{1,0:T(8,128)(2,1)}, bf16[2304,768]{1,0:T(8,128)(2,1)}, f32[16,768]{1,0:T(8,128)}) custom-call(s32[16]{0:T(128)} %group.1, s32[16]{0:T(128)} %lengths.1, bf16[1168,768]{1,0:T(8,128)(2,1)} %tok_h.1, bf16[1168,768]{1,0:T(8,128)(2,1)} %cot_h.1, bf16[3,192,768]{2,1,0:T(8,128)(2,1)} %bitcast.4, ...), custom_call_target="tpu_custom_call" | custom-call | tf_op jit(solution)/shard_map/pallas_call | solution.py:714
  156.1 8.4 %shard_map.264 = (bf16[1168,768]{1,0:T(8,128)(2,1)}, f32[1168,768]{1,0:T(8,128)}, f32[768,768]{1,0:T(8,128)}, f32[768,768]{1,0:T(8,128)}, f32[192,768]{1,0:T(8,1...) custom-call(bf16[1168,768]{1,0:T(8,128)(2,1)} %get-tuple-element.32., ...), custom_call_target="tpu_custom_call" | custom-call | tf_op jit(solution)/shard_map/pallas_call | solution.py:685

commit v3 on v2

--- a/solution.py
+++ b/solution.py
@@ -69,6 +69,51 @@
     for off in range(count // block * block, count, size):
         carry = step(off, carry)
     return carry
+
+
+FIRST, SECOND = (0, 1, 2), (1, 0, 2)
+ORDERS = (FIRST, SECOND, FIRST, FIRST, FIRST, FIRST, FIRST, SECOND)
+PLAN = {
+    "back0": ((0, 0), (1, 0)),
+    "head010": ((2, 0), (0, 1)),
+    "back1": (("early", 0),),
+    "head021": ((2, 1), (3, 0)),
+    "out": (("early", 1), (1, 1), (0, 2)),
+    "head101": (("early", 2),),
+    "head110": ((4, 0), (3, 1), (2, 2)),
+    "head111": (("early", 3),),
+    "head120": ((5, 0),),
+    "head121": ((0, 3), ("early", 4)),
+    "heads": ((1, 2), (4, 1), (6, 0)),
+    "block": ((3, 2), (2, 3), (0, 4), (5, 1), (4, 2)),
+    "grad0": ((1, 3), (7, 0), (5, 2), (6, 1), (2, 4), (3, 3), (7, 1)),
+    "grad1": (
+        (6, 2),
+        (4, 3),
+        ("late", 1),
+        (7, 2),
+        (3, 4),
+        (1, 4),
+        (5, 3),
+        (4, 4),
+        ("late", 2),
+        (7, 3),
+        (6, 3),
+        ("late", 3),
+        (5, 4),
+        ("late", 4),
+        (7, 4),
+        (6, 4),
+    ),
+}
+
+
+def dp_units(width, third):
+    units, start = [], 0
+    for size, order in zip((width // 2,) * 4 + (third,) * 4, ORDERS, strict=True):
+        units.append((start, size, order))
+        start += size
+    return units
 
 
 def layer_kernel(
@@ -110,14 +155,15 @@
     pregrad,
     middle,
     midgrad,
-    mg,
+    keep,
     agrad,
-    dqkv,
-    dacc,
+    dhead,
+    wstack,
+    sgrad,
+    slope,
     tmp_a,
-    tmp_b,
     acc,
-    accv,
+    acch,
     csend,
     crecv,
     ysend,
@@ -125,10 +171,14 @@
     gbuf,
     obuf,
     rx,
+    early,
+    late,
     block,
     ingrad,
-    smc,
-    smr,
+    early_c,
+    early_r,
+    late_c,
+    late_r,
     l_sem,
     w_send,
     w_recv,
@@ -146,7 +196,7 @@
     s_recv,
     *more,
 ):
-    rs, normed2 = more[:12], (more[12:14], more[14:16])
+    rs, normed2, mg = more[:24], (more[24:26], more[26:28]), (more[28:30], more[30:32])
     levels = n_dp.bit_length() - 1
     d = lax.axis_index("dp")
     t = lax.axis_index("tensor")
@@ -206,12 +256,11 @@
         vec[i : i + 1, :] = ref[...][None, :]
     gain1, shift1, bias_out, gain2, shift2, bias_down, bias_up = (vec.at[i : i + 1] for i in range(7))
     acc[...] = jnp.zeros_like(acc)
-    accv[...] = jnp.zeros_like(accv)
+    acch[...] = jnp.zeros_like(acch)
     tok[rows:, :] = jnp.zeros((tok.shape[0] - rows, width), BF)
 
     own, other = 0, HALF
     half_start = (core * HALF, (1 - core) * HALF)
-    lane_head = lax.broadcasted_iota(jnp.int32, (1, third), 1) // HD
     zero8 = jnp.zeros((8, width), F32)
 
     def slot_rows(s, off, size):
@@ -228,27 +277,24 @@
     def y_copy(s, k):
         return remote(ysend.at[s, k], yrecv.at[s, k], y_send.at[s, k], y_recv.at[s, k], y_peer)
 
-    def norm_copy(s):
-        return remote(normed2[s][0], normed2[s][1], g_send.at[s, 0], g_recv.at[s, 0], core_peer)
-
-    def half_copy(ref, s, k):
-        mine, its = slot_rows(s, own, HALF), slot_rows(s, other, HALF)
-        return remote(ref.at[mine], ref.at[its], g_send.at[s, k], g_recv.at[s, k], core_peer)
+    def half_copy(refs, s, k):
+        return remote(refs[s][0], refs[s][1], g_send.at[s, k], g_recv.at[s, k], core_peer)
 
     def gather_copy(ref, s, k):
         region = slot_rows(s, half_start[0], HALF)
         return remote(ref.at[region], ref.at[region], g_send.at[s, k], g_recv.at[s, k], core_peer)
 
-    def stage(s, k, part):
+    def begin(s, k, part):
         csend[...] = part(other).astype(BF)
-        copy = c_copy(s, k)
-        copy.start()
-        tmp_a[...] = part(own)
-        copy.wait()
+        c_copy(s, k).start()
+        keep[...] = part(own)
+
+    def end(s, k):
+        c_copy(s, k).wait()
 
         def add(off, carry):
             r = pl.ds(off, 16)
-            ysend[s, k, r, :] = (tmp_a[r, :] + crecv[s, k, r, :].astype(F32)).astype(BF)
+            ysend[s, k, r, :] = (keep[r, :] + crecv[s, k, r, :].astype(F32)).astype(BF)
             return carry
 
         row_loop(HALF, 16, 6, add, 0)
@@ -257,12 +303,7 @@
     def total(s, k, r):
         return ysend[s, k, r, :].astype(F32) + yrecv[s, k, r, :].astype(F32)
 
-    units = [
-        (0, width, (0, 1, 2)),
-        (width, width, (1, 0, 2)),
-        (2 * width, 2 * third, (0, 1, 2)),
-        (2 * width + 2 * third, 2 * third, (1, 0, 2)),
-    ]
+    units = dp_units(width, third)
 
     def bit(level):
         return (d // 2**level) % 2
@@ -273,62 +314,115 @@
             row0 = row0 + bit(order[i]) * (size >> (i + 1))
         return row0
 
+    def region(u, depth):
+        return pl.ds(pl.multiple_of(base(u, depth), 16), units[u][1] >> depth)
+
     def dp_rs(u, i):
         _, size, order = units[u]
         part = size >> (i + 1)
         src = pl.ds(pl.multiple_of(base(u, i) + (1 - bit(order[i])) * part, 16), part)
         return remote(gbuf.at[src], rs[3 * u + i], d_send.at[u, i], d_recv.at[u, i], dp_peer(order[i]))
 
-    def dp_add(u, i):
-        _, size, _ = units[u]
-        dp_rs(u, i).wait()
-        start = base(u, i + 1)
-        out = obuf if i == 2 else gbuf
+    def dp_swap(u):
+        return remote(gbuf.at[region(u, 2)], rs[3 * u + 2], d_send.at[u, 2], d_recv.at[u, 2], dp_peer(units[u][2][2]))
+
+    def dp_ag(u, i):
+        mine = obuf.at[region(u, i + 1)]
+        return remote(mine, mine, d_send.at[u, 3 + i], d_recv.at[u, 3 + i], dp_peer(units[u][2][i]))
+
+    def dp_add(u, i, out):
+        start = base(u, min(i + 1, 2))
 
         def add(off, carry):
             r = pl.ds(pl.multiple_of(start + off, 16), 16)
             out[r, :] = (gbuf[r, :].astype(F32) + rs[3 * u + i][pl.ds(off, 16), :].astype(F32)).astype(BF)
             return carry
 
-        row_loop(size >> (i + 1), 16, 3, add, 0)
-
-    def dp_extra(u):
-        row0, size, _ = units[u]
-        mine = pl.ds(pl.multiple_of(base(u, 3), 16), size >> 3)
-        spot = pl.ds(row0 >> 3, size >> 3)
+        row_loop(units[u][1] >> min(i + 1, 2), 16, 3, add, 0)
+
+    def dp_further(u):
+        spot = pl.ds(units[u][0] >> 2, units[u][1] >> 2)
         for e in range(levels - 3):
-            copy = remote(obuf.at[mine], rx.at[e, spot], d_send.at[u, 6 + e], d_recv.at[u, 6 + e], dp_peer(3 + e))
+            mine = region(u, 2)
+            copy = remote(obuf.at[mine], rx.at[e, spot], d_send.at[u, 5 + e], d_recv.at[u, 5 + e], dp_peer(3 + e))
             copy.start()
             copy.wait()
             obuf[mine, :] = (obuf[mine, :].astype(F32) + rx[e, spot, :].astype(F32)).astype(BF)
 
-    def dp_ag(u, i):
-        _, size, order = units[u]
-        region = pl.ds(pl.multiple_of(base(u, i + 1), 16), size >> (i + 1))
-        return remote(obuf.at[region], obuf.at[region], d_send.at[u, 3 + i], d_recv.at[u, 3 + i], dp_peer(order[i]))
-
     def dp_out(u):
         row0, size, _ = units[u]
         return local(6 + u, obuf.at[row0 : row0 + size], grads_h.at[row0 : row0 + size])
 
     def advance(u, k):
-        if k < 2:
-            dp_add(u, k)
-            dp_rs(u, k + 1).start()
+        if k == 0:
+            dp_rs(u, 0).wait()
+            dp_add(u, 0, gbuf)
+            dp_rs(u, 1).start()
+        elif k == 1:
+            dp_rs(u, 1).wait()
+            dp_add(u, 1, gbuf)
+            dp_swap(u).start()
         elif k == 2:
-            dp_add(u, 2)
-            dp_extra(u)
-            dp_ag(u, 2).start()
+            dp_swap(u).wait()
+            dp_add(u, 2, obuf)
+            dp_further(u)
+            dp_ag(u, 1).start()
+        elif k == 3:
+            dp_ag(u, 1).wait()
+            dp_ag(u, 0).start()
         else:
-            dp_ag(u, 5 - k).wait()
-            if k < 5:
-                dp_ag(u, 4 - k).start()
+            dp_ag(u, 0).wait()
+            dp_out(u).start()
+
+    def serve(place):
+        for u, k in PLAN.get(place, ()):
+            if u == "early":
+                early_step(k)
+            elif u == "late":
+                late_step(k)
             else:
-                dp_out(u).start()
-
-    def serve(*steps):
-        for u, k in steps:
-            advance(u, k)
+                advance(u, k)
+
+    def exchange(buf, landing, sem, peer):
+        return remote(buf, landing, s_send.at[sem], s_recv.at[sem], peer)
+
+    def early_step(k):
+        if k == 0:
+            early[...] = jnp.zeros_like(early)
+            for i in range(4):
+                early[i : i + 1, :] = jnp.sum(acc[2 + i], axis=0, keepdims=True)
+            exchange(early, early_c, 0, core_peer).start()
+            return
+        landing = early_c if k == 1 else early_r.at[k - 2]
+        exchange(early, landing, k - 1, core_peer if k == 1 else dp_peer(k - 2)).wait()
+        early[...] = early[...] + landing[...]
+        if k == 1:
+            early[4:5, :] = jnp.sum(acc[6], axis=0, keepdims=True)
+        if k <= levels:
+            exchange(early, early_r.at[k - 1], k, dp_peer(k - 1)).start()
+
+    tiles = width // 128
+
+    def late_step(k):
+        first = 1 + levels
+        if k == 0:
+            late[...] = jnp.zeros_like(late)
+            for i in range(2):
+                row = jnp.sum(acc[i], axis=0, keepdims=True)
+                for j in range(tiles):
+                    late[i * tiles + j : i * tiles + j + 1, :] = row[:, j * 128 : (j + 1) * 128]
+            exchange(late, late_c, first, core_peer).start()
+            return
+        landing = late_c if k == 1 else late_r.at[k - 2]
+        exchange(late, landing, first + k - 1, core_peer if k == 1 else dp_peer(k - 2)).wait()
+        late[...] = late[...] + landing[...]
+        if k == 1:
+            for h in range(heads):
+                row = jnp.sum(acch[h], axis=0, keepdims=True)
+                late[2 * tiles + h : 2 * tiles + h + 1, 0:HD] = row[:, 0:HD]
+                late[2 * tiles + h : 2 * tiles + h + 1, HD : 2 * HD] = row[:, 2 * HD : 3 * HD]
+        if k <= levels:
+            exchange(late, late_r.at[k - 1], first + k, dp_peer(k - 1)).start()
 
     def norm_rows(s):
         for half, start in enumerate(half_start):
@@ -364,6 +458,9 @@
         copy.start()
     loads[1].wait()
     norm_rows(1)
+    for h in range(heads):
+        for j in range(3):
+            wstack[h, j * HD : (j + 1) * HD, :] = wqkv[j, h * HD : (h + 1) * HD, :]
 
     def a_swap(s):
         return remote(att.at[slot_rows(s, other, HALF)], attc.at[s], a_send.at[s, 0], a_recv.at[s, 0], core_peer)
@@ -371,8 +468,8 @@
     def a_copy(s):
         return remote(attf.at[s, side], attf.at[s, side], a_send.at[s, 1], a_recv.at[s, 1], y_peer)
 
-    def forward_attention(s, carry):
-        def project(i, carry):
+    def project(s):
+        def half(i, carry):
             r = slot_rows(s, i * HALF, HALF)
             x = normed[r, :]
             qkv[0, r, :] = (dot_nt(x, wqkv[0]) + qvb[0:1, :]).astype(BF)
@@ -380,40 +477,47 @@
             qkv[2, r, :] = (dot_nt(x, wqkv[2]) + qvb[1:2, :]).astype(BF)
             return carry
 
-        lax.fori_loop(0, 2, project, 0)
+        lax.fori_loop(0, 2, half, 0)
+
+    def attend(s):
         whole = slot_rows(s, 0, SLOT)
         key = lax.broadcasted_iota(jnp.int32, (1, SLOT), 1)
         key = key + jnp.where(key < HALF, half_start[0], half_start[1] - HALF)
         key_bias = jnp.where(inside(s, key), 0.0, MASKED)
 
-        def attend(i, carry):
+        def half(i, carry):
             r = slot_rows(s, i * HALF, HALF)
             for h in range(heads):
-                q = jnp.where(lane_head == h, qkv[0, r, :] * HD**-0.5, 0.0).astype(BF)
-                scores = dot_nt(q, qkv[1, whole, :]) + key_bias
+                lanes = slice(h * HD, (h + 1) * HD)
+                q = (qkv[0, r, lanes] * HD**-0.5).astype(BF)
+                scores = dot_nt(q, qkv[1, whole, lanes]) + key_bias
                 exps = jnp.exp(scores - jnp.max(scores, axis=-1, keepdims=True))
                 weights = (exps * (1.0 / jnp.sum(exps, axis=-1, keepdims=True))).astype(BF)
                 probs[s * heads + h, pl.ds(pl.multiple_of(i * HALF, 16), HALF), :] = weights
-                part = dot_nn(weights, qkv[2, whole, :])
-                result = part if h == 0 else jnp.where(lane_head == h, part, result)
-            att[r, :] = result.astype(BF)
+                att[r, lanes] = dot_nn(weights, qkv[2, whole, lanes]).astype(BF)
             return carry
 
-        lax.fori_loop(0, 2, attend, 0)
+        lax.fori_loop(0, 2, half, 0)
         a_swap(s).start()
+
+    def join(s):
         a_swap(s).wait()
         mine, its = att[slot_rows(s, own, HALF), :], attc[s]
         left = jnp.where(core == 0, mine, its)
         right = jnp.where(core == 0, its, mine)
         attf[s, side] = jnp.concatenate([left, right], axis=1)
         a_copy(s).start()
-        return carry
-
-    lax.fori_loop(0, 2, forward_attention, 0)
+
+    project(0)
+    attend(0)
+    project(1)
+    join(0)
+    attend(1)
     w_own[1].wait()
     w_pass.start()
     loads[3].wait()
     mask_rows(0)
+    join(1)
     mask_rows(1)
     w_own[0].wait()
     w_pass.wait()
@@ -433,58 +537,70 @@
             return carry
 
         row_loop(HALF, 16, 6, step, 0)
-        norm_copy(s).start()
-
-    def feed_forward(s):
-        second_norm(s)
-
-        def half(start):
-            r = slot_rows(s, start, HALF)
-            tmp_a[...] = dot_nn(normed2[s][start // HALF][...], wup[...])
-            tmp_b[...] = dot_nt(cot[r, :], wdown[...])
-
-            def step(off, sums):
-                rr = pl.ds(off, 16)
-                g = slot_rows(s, start + off, 16)
-                x = tmp_a[rr, :] + bias_up[...]
-                phi = 0.5 + 0.5 * lax.erf(x * 0.7071067811865476)
-                hidden[g, :] = (x * phi).astype(BF)
-                slope = phi + x * (jnp.exp(x * x * -0.5) * 0.3989422804014327)
-                low = (tmp_b[rr, :] * slope).astype(BF)
-                pregrad[g, :] = low
-                return sums + fold8(low.astype(F32))
-
-            acc[6] += row_loop(HALF, 16, 1, step, zero8)
-
-        half(own)
-        norm_copy(s).wait()
-        half(other)
-        stage(s, 0, lambda off: dot_nt(pregrad[slot_rows(s, off, HALF), :], wup[...]))
-
-    feed_forward(0)
-    feed_forward(1)
-
-    def weight_grad(u, left, right):
-        row0, size, order = units[u]
-        for mine in (0, 1):
-            off = (bit(order[0]) if mine else 1 - bit(order[0])) * (size // 2)
-
-            columns = left(pl.ds(pl.multiple_of(off, 128), size // 2))
-            gbuf[pl.ds(pl.multiple_of(row0 + off, 16), size // 2), :] = dot_tn(columns, right[...]).astype(BF)
-            if not mine:
-                dp_rs(u, 0).start()
+        half_copy(normed2, s, 0).start()
+
+    def up_half(s, half):
+        tmp_a[...] = dot_nn(normed2[s][half][...], wup[...])
+
+        def step(off, carry):
+            g = slot_rows(s, half * HALF + off, 16)
+            x = tmp_a[pl.ds(off, 16), :] + bias_up[...]
+            phi = 0.5 + 0.5 * lax.erf(x * 0.7071067811865476)
+            hidden[g, :] = (x * phi).astype(BF)
+            slope[g, :] = phi + x * (jnp.exp(x * x * -0.5) * 0.3989422804014327)
+            return carry
+
+        row_loop(HALF, 16, 2, step, 0)
+
+    def back_half(s, half):
+        tmp_a[...] = dot_nt(cot[slot_rows(s, half * HALF, HALF), :], wdown[...])
+
+        def step(off, sums):
+            g = slot_rows(s, half * HALF + off, 16)
+            low = (tmp_a[pl.ds(off, 16), :] * slope[g, :]).astype(BF)
+            pregrad[g, :] = low
+            return sums + fold8(low.astype(F32))
+
+        acc[6] += row_loop(HALF, 16, 6, step, zero8)
+
+    def unit_grad(u, left, right):
+        row0, size, _ = units[u]
+        gbuf[row0 : row0 + size, :] = dot_tn(left, right[...]).astype(BF)
+        dp_rs(u, 0).start()
 
     def norm_columns(columns):
         return jnp.concatenate([ref[:, columns] for refs in normed2 for ref in refs], axis=0)
 
-    weight_grad(0, lambda columns: hidden[:, columns], cot)
-    weight_grad(1, norm_columns, pregrad)
-
-    def feed_forward_out(s, carry):
-        stage(s, 1, lambda off: dot_nn(hidden[slot_rows(s, off, HALF), :], wdown[...]))
-        return carry
-
-    lax.fori_loop(0, 2, feed_forward_out, 0)
+    lower, upper = slice(0, width // 2), slice(width // 2, width)
+    def norm_part(s):
+        begin(s, 0, lambda off: dot_nt(pregrad[slot_rows(s, off, HALF), :], wup[...]))
+
+    def out_part(s):
+        begin(s, 1, lambda off: dot_nn(hidden[slot_rows(s, off, HALF), :], wdown[...]))
+
+    second_norm(0)
+    up_half(0, 0)
+    half_copy(normed2, 0, 0).wait()
+    up_half(0, 1)
+    back_half(0, 1)
+    back_half(0, 0)
+    norm_part(0)
+    second_norm(1)
+    end(0, 0)
+    up_half(1, 0)
+    half_copy(normed2, 1, 0).wait()
+    up_half(1, 1)
+    unit_grad(0, hidden[:, lower], cot)
+    unit_grad(1, hidden[:, upper], cot)
+    back_half(1, 1)
+    back_half(1, 0)
+    norm_part(1)
+    unit_grad(2, norm_columns(lower), pregrad)
+    end(1, 0)
+    out_part(0)
+    unit_grad(3, norm_columns(upper), pregrad)
+    end(0, 1)
+    out_part(1)
 
     def second_back(s):
         y_copy(s, 0).wait()
@@ -497,7 +613,7 @@
             og = cot[g, :].astype(F32)
             m = og + norm_back(n * gain2[...], xn, scale)
             midgrad[s, r, :] = m
-            mg[g, :] = m.astype(BF)
+            mg[s][0][r, :] = m.astype(BF)
             return tuple(a + fold8(b) for a, b in zip(sums, (n * xn, n, m, og), strict=True))
 
         sums = row_loop(HALF, 16, 3, step, (zero8,) * 4)
@@ -505,57 +621,59 @@
             acc[2 + i] += sums[i]
         half_copy(mg, s, 1).start()
 
-    def attention_back(s, services):
-        second_back(s)
+    def head_back(s, h):
+        whole = slot_rows(s, 0, SLOT)
+        lanes = slice(h * HD, (h + 1) * HD)
+        keys, values = qkv[1, whole, lanes], qkv[2, whole, lanes]
+        for c in (0, 1):
+            r = slot_rows(s, c * HALF, HALF)
+            part = slice(c * HALF, (c + 1) * HALF)
+            p = probs[s * heads + h, part, :].astype(F32)
+            prob_grad = dot_nt(agrad[r, lanes], values)
+            inner = jnp.sum(p * prob_grad, axis=-1, keepdims=True)
+            sgrad[part, :] = (p * (prob_grad - inner)).astype(BF)
+            dhead[h, r, 0:HD] = (dot_nn(sgrad[part, :], keys) * HD**-0.5).astype(BF)
+            serve(f"head{s}{h}{c}")
+        dhead[h, whole, HD : 2 * HD] = (dot_tn(sgrad[...], qkv[0, whole, lanes]) * HD**-0.5).astype(BF)
+        dhead[h, whole, 2 * HD : 3 * HD] = dot_tn(probs[s * heads + h], agrad[whole, lanes]).astype(BF)
+        acch[h] += fold8(dhead[h, whole, :].astype(F32))
+
+    def attended_grad(s):
         half_copy(mg, s, 1).wait()
-        whole = slot_rows(s, 0, SLOT)
-        agrad[whole, :] = dot_nt(mg[whole, :], wout[my_quarter, :]).astype(BF)
-        dacc[...] = jnp.zeros_like(dacc)
-
-        def chunk(i):
-            r = slot_rows(s, i * HALF, HALF)
-            for h in range(heads):
-                mask = lane_head == h
-                do = agrad[r, :]
-                w = probs[s * heads + h, pl.ds(pl.multiple_of(i * HALF, 16), HALF), :]
-                prob_grad = dot_nt(jnp.where(mask, do, 0.0).astype(BF), qkv[2, whole, :])
-                p = w.astype(F32)
-                inner = jnp.sum(p * prob_grad, axis=-1, keepdims=True)
-                score_grad = (p * (prob_grad - inner)).astype(BF)
-                part = dot_nn(score_grad, qkv[1, whole, :])
-                dq = part if h == 0 else jnp.where(mask, part, dq)
-                dacc[0] += jnp.where(mask, dot_tn(score_grad, qkv[0, r, :]), 0.0)
-                dacc[1] += jnp.where(mask, dot_tn(w, do), 0.0)
-            low = (dq * HD**-0.5).astype(BF)
-            dqkv[0, r, :] = low
-            accv[0] += fold8(low.astype(F32))
-
-            serve(*services[i])
-
-        chunk(0)
-        chunk(1)
-        dqkv[1, whole, :] = (dacc[0] * HD**-0.5).astype(BF)
-        low = dacc[1].astype(BF)
-        dqkv[2, whole, :] = low
-        accv[1] += fold8(low.astype(F32))
-
+        agrad[slot_rows(s, 0, SLOT), :] = dot_nt(
+            jnp.concatenate([mg[s][0][...], mg[s][1][...]], axis=0), wout[my_quarter, :]
+        ).astype(BF)
+
+    def projected(s):
         def part(off):
             r = slot_rows(s, off, HALF)
-            return dot_nn(dqkv[0, r, :], wqkv[0]) + dot_nn(dqkv[1, r, :], wqkv[1]) + dot_nn(dqkv[2, r, :], wqkv[2])
-
-        stage(s, 2, part)
-
-    attention_back(0, (((0, 0),), ((1, 0),)))
-    attention_back(1, (((0, 1), (1, 1)), ((0, 2), (1, 2))))
-
-    low0 = 2 * width
-    gbuf[low0 : low0 + third, :] = dot_tn(att[...], mg[...]).astype(BF)
-    gbuf[low0 + third : low0 + 2 * third, :] = dot_tn(dqkv[0], normed[...]).astype(BF)
-    dp_rs(2, 0).start()
-    gbuf[low0 + 2 * third : low0 + 3 * third, :] = dot_tn(dqkv[1], normed[...]).astype(BF)
-    gbuf[low0 + 3 * third : low0 + 4 * third, :] = dot_tn(dqkv[2], normed[...]).astype(BF)
-    dp_rs(3, 0).start()
-    serve((0, 3), (1, 3))
+            return sum(dot_nn(dhead[h, r, :], wstack[h]) for h in range(heads))
+
+        begin(s, 2, part)
+
+    second_back(0)
+    end(1, 1)
+    serve("back0")
+    attended_grad(0)
+    for h in range(heads - 1):
+        head_back(0, h)
+    second_back(1)
+    serve("back1")
+    head_back(0, heads - 1)
+    projected(0)
+    attended_grad(1)
+    end(0, 2)
+    all_mg = jnp.concatenate([ref[...] for refs in mg for ref in refs], axis=0)
+    gbuf[2 * width : 2 * width + third, :] = dot_tn(att[...], all_mg).astype(BF)
+    dp_rs(4, 0).start()
+    serve("out")
+    for h in range(heads):
+        head_back(1, h)
+        if h == heads - 1:
+            projected(1)
+        unit_grad(5 + h, dhead[h], normed)
+    serve("heads")
+    end(1, 2)
 
     def finish_block(s):
         y_copy(s, 1).wait()
@@ -600,59 +718,53 @@
 
         row_loop(rows, 16, 1, step, 0)
 
-    serve((2, 0), (3, 0))
     finish_block(0)
-    serve((0, 4), (1, 4), (2, 1), (3, 1))
     finish_block(1)
-    serve((0, 5), (1, 5), (2, 2), (3, 2))
     for s in (0, 1):
         gather_copy(block, s, 2).wait()
     assemble(block)
-    out_block = local(10, block.at[0:rows], block_h)
+    out_block = local(14, block.at[0:rows], block_h)
     out_block.start()
-    serve((2, 3), (3, 3))
+    serve("block")
     finish_grad(0)
-    serve((2, 4), (3, 4))
+    serve("grad0")
     finish_grad(1)
-
-    for i in range(7):
-        row = i if i < 6 else 8
-        small_o[row : row + 1, :] = jnp.sum(acc[i], axis=0, keepdims=True)
-    small_o[6:8, :] = jnp.zeros((2, width), F32)
-    small_o[9:16, :] = jnp.zeros((7, width), F32)
-    for i in range(2):
-        small_o[9 + i : 10 + i, 0:third] = jnp.sum(accv[i], axis=0, keepdims=True)
-    copy = remote(small_o.at[0:8], smc, s_send.at[0], s_recv.at[0], core_peer)
-    copy.start()
-    copy.wait()
-    small_o[0:8, :] = small_o[0:8, :] + smc[...]
-    copy = remote(small_o, smr.at[0], s_send.at[1], s_recv.at[1], dp_peer(0))
-    copy.start()
+    late_step(0)
     for s in (0, 1):
         gather_copy(ingrad, s, 3).wait()
     assemble(ingrad)
-    out_grad = local(11, ingrad.at[0:rows], ingrad_h)
+    out_grad = local(15, ingrad.at[0:rows], ingrad_h)
     out_grad.start()
-    for i in range(levels):
-        if i:
-            copy = remote(small_o, smr.at[i], s_send.at[1 + i], s_recv.at[1 + i], dp_peer(i))
-            copy.start()
-        copy.wait()
-        small_o[...] = small_o[...] + smr[i]
-    serve((2, 5), (3, 5))
+    serve("grad1")
+    for k in range(5, levels + 2):
+        early_step(k)
+        late_step(k)
+
+    small_o[...] = jnp.zeros_like(small_o)
+    for i in range(2):
+        for j in range(tiles):
+            small_o[i : i + 1, j * 128 : (j + 1) * 128] = late[i * tiles + j : i * tiles + j + 1, :]
+    small_o[2:6, :] = early[0:4, :]
+    small_o[8:9, :] = early[4:5, :]
+    for h in range(heads):
+        row = late[2 * tiles + h : 2 * tiles + h + 1, :]
+        small_o[9:10, h * HD : (h + 1) * HD] = row[:, 0:HD]
+        small_o[10:11, h * HD : (h + 1) * HD] = row[:, HD : 2 * HD]
     out_block.wait()
     out_grad.wait()
-    for u in range(4):
+    for u in range(len(units)):
         dp_out(u).wait()
 
 
-def unpack_kernel(block, ingrad, down, up, out, qkv, small, *outs):
+def unpack_kernel(block, ingrad, down, up, out, qkv0, qkv1, qkv2, small, *outs):
     outs[0][...] = block[...]
     outs[1][...] = ingrad[...].astype(F32)
     outs[2][...] = down[...].astype(F32)
     outs[3][...] = up[...].astype(F32)
     outs[4][...] = out[...].astype(F32)
-    outs[5][...] = qkv[...].astype(F32)
+    for i, qkv in enumerate((qkv0, qkv1, qkv2)):
+        rows = qkv.shape[0]
+        outs[5][i * rows : (i + 1) * rows, :] = qkv[...].astype(F32)
 
     @pl.when(pl.program_id(0) == 0)
     def _():
@@ -673,6 +785,15 @@
         return pl.BlockSpec(shape, lambda i: (0,) * len(shape))
 
     big, mid, low = width // steps, 3 * third // steps, third // steps
+    piece = mid // 3
+    per_head = HD // piece
+
+    def qkv_part(b, i):
+        m = 3 * i + b
+        kind, rest = m // (third // piece), m % (third // piece)
+        head, low_part = rest // per_head, rest % per_head
+        return (2 * width + third) // piece + (head * 3 + kind) * per_head + low_part, 0
+
     shapes = [
         ((rows, width), BF, part(row_block, 0)),
         ((rows, width), F32, part(row_block, 0)),
@@ -692,11 +813,11 @@
             part(big, 0),
             part(big, width),
             part(low, 2 * width),
-            part(mid, 2 * width + third),
+            *(pl.BlockSpec((piece, width), functools.partial(qkv_part, b)) for b in range(3)),
             whole(small.shape),
         ],
         out_specs=[spec for _, _, spec in shapes],
-    )(block, ingrad, grads, grads, grads, grads, small)
+    )(block, ingrad, grads, grads, grads, grads, grads, grads, small)
 
 
 def call_layer(n_dp, *operands):
@@ -739,26 +860,31 @@
             pltpu.VMEM((slots, width), BF),
             pltpu.VMEM((2, HALF, width), F32),
             pltpu.VMEM((2, HALF, width), F32),
-            pltpu.VMEM((slots, width), BF),
+            pltpu.VMEM((HALF, width), F32),
             pltpu.VMEM((slots, third), BF),
-            pltpu.VMEM((3, slots, third), BF),
-            pltpu.VMEM((2, SLOT, third), F32),
-            pltpu.VMEM((HALF, width), F32),
+            pltpu.VMEM((heads, slots, third), BF),
+            pltpu.VMEM((heads, third, width), BF),
+            pltpu.VMEM((SLOT, SLOT), BF),
+            pltpu.VMEM((slots, width), F32),
             pltpu.VMEM((HALF, width), F32),
             pltpu.VMEM((7, 8, width), F32),
-            pltpu.VMEM((2, 8, third), F32),
+            pltpu.VMEM((heads, 8, third), F32),
             pltpu.VMEM((HALF, width), BF),
             pltpu.VMEM((2, 3, HALF, width), BF),
             pltpu.VMEM((2, 3, HALF, width), BF),
             pltpu.VMEM((2, 3, HALF, width), BF),
             pltpu.VMEM((grad_rows, width), BF),
             pltpu.VMEM((grad_rows, width), BF),
-            pltpu.VMEM((extra, grad_rows // 8, width), BF),
+            pltpu.VMEM((extra, grad_rows // 4 if levels > 3 else 16, width), BF),
+            pltpu.VMEM((8, width), F32),
+            pltpu.VMEM((16, 128), F32),
             pltpu.VMEM((slots, width), BF),
             pltpu.VMEM((slots, width), BF),
             pltpu.VMEM((8, width), F32),
-            pltpu.VMEM((levels, 16, width), F32),
-            dma((12,)),
+            pltpu.VMEM((levels, 8, width), F32),
+            pltpu.VMEM((16, 128), F32),
+            pltpu.VMEM((levels, 16, 128), F32),
+            dma((16,)),
             dma((3,)),
             dma((3,)),
             dma((2, 2)),
@@ -769,13 +895,13 @@
             dma((2, 3)),
             dma((2, 4)),
             dma((2, 4)),
-            dma((4, 6 + extra)),
-            dma((4, 6 + extra)),
-            dma((1 + levels,)),
-            dma((1 + levels,)),
+            dma((8, 5 + extra)),
+            dma((8, 5 + extra)),
+            dma((2 + 2 * levels,)),
+            dma((2 + 2 * levels,)),
         ]
-        + [pltpu.VMEM((size >> (i + 1), width), BF) for size in (width, width, 2 * third, 2 * third) for i in range(3)]
-        + [pltpu.VMEM((HALF, width), BF)] * 4,
+        + [pltpu.VMEM((size >> min(i + 1, 2), width), BF) for _, size, _ in dp_units(width, third) for i in range(3)]
+        + [pltpu.VMEM((HALF, width), BF)] * 8,
         compiler_params=pltpu.CompilerParams(
             collective_id=0, has_side_effects=True, vmem_limit_bytes=67043328
         ),

time: 165 us -> 133 us (0.81)
  Pallas kernels: 164 us -> 132 us
    pallas_call x1, Pallas kernels: 155 us -> 123 us  [call_layer(): pl.pallas_call(functools.partial(layer_kernel, n_dp), out_shape=(jax.Shap...]
where the time goes in v3:
time: 133 us
  Pallas kernels  132 us (99%)
    pallas_call x1, Pallas kernels, call_layer(): pl.pallas_call(functools.partial(layer_kernel, n_dp), out_shape=(jax.Shap...  123 us
    pallas_call x1, Pallas kernels, call_unpack(): pl.pallas_call(unpack_kernel, grid=(steps,), out_shape=[jax.ShapeDtypeStr...  8.55 us

profile of v3, /device:TPU:0, one launch (start us, length us, event | category | flops | bytes accessed | tf_op | source)
XLA Modules:
  0.0 132.5 jit_solution(4361140882066248027)
XLA Ops:
  0.7 123.1 %shard_map.263 = (bf16[1168,768]{1,0:T(8,128)(2,1)}, bf16[1168,768]{1,0:T(8,128)(2,1)}, bf16[2304,768]{1,0:T(8,128)(2,1)}, f32[16,768]{1,0:T(8,128)}) custom-call(s32[16]{0:T(128)} %group.1, s32[16]{0:T(128)} %lengths.1, bf16[1168,768]{1,0:T(8,128)(2,1)} %tok_h.1, bf16[1168,768]{1,0:T(8,128)(2,1)} %cot_h.1, bf16[3,192,768]{2,1,0:T(8,128)(2,1)} %bitcast.4, ...), custom_call_target="tpu_custom_call" | custom-call | tf_op jit(solution)/shard_map/pallas_call | solution.py:835
  123.8 8.6 %shard_map.264 = (bf16[1168,768]{1,0:T(8,128)(2,1)}, f32[1168,768]{1,0:T(8,128)}, f32[768,768]{1,0:T(8,128)}, f32[768,768]{1,0:T(8,128)}, f32[192,768]{1,0:T(8,1...) custom-call(bf16[1168,768]{1,0:T(8,128)(2,1)} %get-tuple-element.32., ...), custom_call_target="tpu_custom_call" | custom-call | tf_op jit(solution)/shard_map/pallas_call | solution.py:806

commit v4 on v3

--- a/solution.py
+++ b/solution.py
@@ -194,6 +194,7 @@
     d_recv,
     s_send,
     s_recv,
+    ready,
     *more,
 ):
     rs, normed2, mg = more[:24], (more[24:26], more[26:28]), (more[28:30], more[30:32])
@@ -341,13 +342,15 @@
         row_loop(units[u][1] >> min(i + 1, 2), 16, 3, add, 0)
 
     def dp_further(u):
-        spot = pl.ds(units[u][0] >> 2, units[u][1] >> 2)
+        size, mine = units[u][1] >> 2, region(u, 2)
         for e in range(levels - 3):
-            mine = region(u, 2)
-            copy = remote(obuf.at[mine], rx.at[e, spot], d_send.at[u, 5 + e], d_recv.at[u, 5 + e], dp_peer(3 + e))
+            peer = dp_peer(3 + e)
+            pl.semaphore_signal(ready.at[e], inc=1, device_id=peer, device_id_type=MESH)
+            pl.semaphore_wait(ready.at[e], 1)
+            copy = remote(obuf.at[mine], rx.at[0:size], d_send.at[u, 5 + e], d_recv.at[u, 5 + e], peer)
             copy.start()
             copy.wait()
-            obuf[mine, :] = (obuf[mine, :].astype(F32) + rx[e, spot, :].astype(F32)).astype(BF)
+            obuf[mine, :] = (obuf[mine, :].astype(F32) + rx[0:size, :].astype(F32)).astype(BF)
 
     def dp_out(u):
         row0, size, _ = units[u]
@@ -875,7 +878,7 @@
             pltpu.VMEM((2, 3, HALF, width), BF),
             pltpu.VMEM((grad_rows, width), BF),
             pltpu.VMEM((grad_rows, width), BF),
-            pltpu.VMEM((extra, grad_rows // 4 if levels > 3 else 16, width), BF),
+            pltpu.VMEM((width // 8 if levels > 3 else 16, width), BF),
             pltpu.VMEM((8, width), F32),
             pltpu.VMEM((16, 128), F32),
             pltpu.VMEM((slots, width), BF),
@@ -899,6 +902,7 @@
             dma((8, 5 + extra)),
             dma((2 + 2 * levels,)),
             dma((2 + 2 * levels,)),
+            pltpu.SemaphoreType.REGULAR((extra,)),
         ]
         + [pltpu.VMEM((size >> min(i + 1, 2), width), BF) for _, size, _ in dp_units(width, third) for i in range(3)]
         + [pltpu.VMEM((HALF, width), BF)] * 8,

time: 133 us -> 133 us (level)
  no operation moved by 1% of the time
where the time goes in v4:
time: 133 us
  Pallas kernels  132 us (99%)
    pallas_call x1, Pallas kernels, call_layer(): pl.pallas_call(functools.partial(layer_kernel, n_dp), out_shape=(jax.Shap...  123 us
    pallas_call x1, Pallas kernels, call_unpack(): pl.pallas_call(unpack_kernel, grid=(steps,), out_shape=[jax.ShapeDtypeStr...  8.55 us

profile of v4, /device:TPU:0, one launch (start us, length us, event | category | flops | bytes accessed | tf_op | source)
XLA Modules:
  0.0 132.5 jit_solution(4098237199539456756)
XLA Ops:
  0.7 123.1 %shard_map.263 = (bf16[1168,768]{1,0:T(8,128)(2,1)}, bf16[1168,768]{1,0:T(8,128)(2,1)}, bf16[2304,768]{1,0:T(8,128)(2,1)}, f32[16,768]{1,0:T(8,128)}) custom-call(s32[16]{0:T(128)} %group.1, s32[16]{0:T(128)} %lengths.1, bf16[1168,768]{1,0:T(8,128)(2,1)} %tok_h.1, bf16[1168,768]{1,0:T(8,128)(2,1)} %cot_h.1, bf16[3,192,768]{2,1,0:T(8,128)(2,1)} %bitcast.4, ...), custom_call_target="tpu_custom_call" | custom-call | tf_op jit(solution)/shard_map/pallas_call | solution.py:838
  123.8 8.6 %shard_map.264 = (bf16[1168,768]{1,0:T(8,128)(2,1)}, f32[1168,768]{1,0:T(8,128)}, f32[768,768]{1,0:T(8,128)}, f32[768,768]{1,0:T(8,128)}, f32[192,768]{1,0:T(8,1...) custom-call(bf16[1168,768]{1,0:T(8,128)(2,1)} %get-tuple-element.32., ...), custom_call_target="tpu_custom_call" | custom-call | tf_op jit(solution)/shard_map/pallas_call | solution.py:809

commit v5 on v4

--- a/solution.py
+++ b/solution.py
@@ -75,9 +75,11 @@
 ORDERS = (FIRST, SECOND, FIRST, FIRST, FIRST, FIRST, FIRST, SECOND)
 PLAN = {
     "back0": ((0, 0), (1, 0)),
-    "head010": ((2, 0), (0, 1)),
+    "head001": ((2, 0),),
+    "head010": ((0, 1),),
     "back1": (("early", 0),),
-    "head021": ((2, 1), (3, 0)),
+    "head011": ((3, 0),),
+    "head020": ((2, 1),),
     "out": (("early", 1), (1, 1), (0, 2)),
     "head101": (("early", 2),),
     "head110": ((4, 0), (3, 1), (2, 2)),
@@ -85,8 +87,8 @@
     "head120": ((5, 0),),
     "head121": ((0, 3), ("early", 4)),
     "heads": ((1, 2), (4, 1), (6, 0)),
-    "block": ((3, 2), (2, 3), (0, 4), (5, 1), (4, 2)),
-    "grad0": ((1, 3), (7, 0), (5, 2), (6, 1), (2, 4), (3, 3), (7, 1)),
+    "block": ((5, 1), (3, 2), (2, 3), (4, 2), (0, 4)),
+    "grad0": ((7, 0), (1, 3), (6, 1), (5, 2), (3, 3), (7, 1), (2, 4)),
     "grad1": (
         (6, 2),
         (4, 3),
@@ -245,8 +247,10 @@
     second_skip = jnp.where(first_small, RES_SMALL % 16, RES_LARGE % 16)
 
     def group_rows(ref, s, off, size):
-        small = ref[pl.ds(pl.multiple_of(s * SMALL_START + off, 16), size), :].astype(F32)
-        large = ref[pl.ds(pl.multiple_of(s * LARGE_START + off, 16), size), :].astype(F32)
+        if s == 0:
+            return ref[pl.ds(pl.multiple_of(off, 16), size), :].astype(F32)
+        small = ref[pl.ds(pl.multiple_of(SMALL_START + off, 16), size), :].astype(F32)
+        large = ref[pl.ds(pl.multiple_of(LARGE_START + off, 16), size), :].astype(F32)
         return jnp.where(first_small, small, large)
 
     def inside(s, index):

time: 133 us -> 131 us (0.985)
  Pallas kernels: 132 us -> 130 us
    pallas_call x1, Pallas kernels: 123 us -> 121 us  [call_layer(): pl.pallas_call(functools.partial(layer_kernel, n_dp), out_shape=(jax.Shap...]
where the time goes in v5:
time: 131 us
  Pallas kernels  130 us (99%)
    pallas_call x1, Pallas kernels, call_layer(): pl.pallas_call(functools.partial(layer_kernel, n_dp), out_shape=(jax.Shap...  121 us
    pallas_call x1, Pallas kernels, call_unpack(): pl.pallas_call(unpack_kernel, grid=(steps,), out_shape=[jax.ShapeDtypeStr...  8.55 us

profile of v5, /device:TPU:0, one launch (start us, length us, event | category | flops | bytes accessed | tf_op | source)
XLA Modules:
  0.0 130.8 jit_solution(10598881028244750491)
XLA Ops:
  0.7 121.4 %shard_map.263 = (bf16[1168,768]{1,0:T(8,128)(2,1)}, bf16[1168,768]{1,0:T(8,128)(2,1)}, bf16[2304,768]{1,0:T(8,128)(2,1)}, f32[16,768]{1,0:T(8,128)}) custom-call(s32[16]{0:T(128)} %group.1, s32[16]{0:T(128)} %lengths.1, bf16[1168,768]{1,0:T(8,128)(2,1)} %tok_h.1, bf16[1168,768]{1,0:T(8,128)(2,1)} %cot_h.1, bf16[3,192,768]{2,1,0:T(8,128)(2,1)} %bitcast.4, ...), custom_call_target="tpu_custom_call" | custom-call | tf_op jit(solution)/shard_map/pallas_call | solution.py:842
  122.1 8.6 %shard_map.264 = (bf16[1168,768]{1,0:T(8,128)(2,1)}, f32[1168,768]{1,0:T(8,128)}, f32[768,768]{1,0:T(8,128)}, f32[768,768]{1,0:T(8,128)}, f32[192,768]{1,0:T(8,1...) custom-call(bf16[1168,768]{1,0:T(8,128)(2,1)} %get-tuple-element.32., ...), custom_call_target="tpu_custom_call" | custom-call | tf_op jit(solution)/shard_map/pallas_call | solution.py:813
